TPU v7x, 32 devices: a whole 2x2x4 slice. The times are simulated.
32 devices in a mesh: dp: 16 (over z, y, core), tensor: 2 (over x).
Axes of the slice: x: 2, y: 2, z: 4, core: 2. Of those that a mesh axis runs over, the one named last changes fastest.
Arguments:
- tokens: bfloat16 [16, 1024, 768], P(None, 'dp', 'tensor'), may hold values from -6 to 6
- cotangent: bfloat16 [16, 1024, 768], P(None, 'dp', 'tensor'), may hold values from -6 to 6
- thoughts: bfloat16 [16, 6, 768], P('dp', None, 'tensor'), may hold values from -6 to 6
- latent_pos: int32 [16, 6], P('dp'), may hold values from 1 to 63, as said below
- lengths: int32 [16], replicated, may hold values from 64 to 1024, as said below
- dealing: int32 [16], replicated, may hold values from 0 to 15, each once
- qkv_weight: bfloat16 [3, 768, 768], P(None, None, 'tensor'), may hold values from -0.21875 to 0.21875
- qv_bias: float32 [2, 768], P(None, 'tensor'), may hold values from -3 to 3
- out_weight: bfloat16 [768, 768], P('tensor'), may hold values from -0.875 to 0.875
- out_bias: float32 [2, 768], replicated, may hold values from -3 to 3
- fc_weight: bfloat16 [768, 3072], P(None, 'tensor'), may hold values from -0.21875 to 0.21875
- fc_bias: float32 [3072], P('tensor'), may hold values from -3 to 3
- proj_weight: bfloat16 [3072, 768], P('tensor'), may hold values from -0.109375 to 0.109375
- norm_gain: float32 [2, 768], replicated, may hold values from 0.5 to 1.5
- norm_shift: float32 [2, 768], replicated, may hold values from -3 to 3
Outputs:
- block_out: float32 [16, 1024, 768], P(None, 'dp', 'tensor')
- input_grad: float32 [16, 1024, 768], P(None, 'dp', 'tensor')
- grad_qkv_weight: float32 [3, 768, 768], P(None, None, 'tensor')
- grad_qv_bias: float32 [2, 768], P(None, 'tensor')
- grad_out_weight: float32 [768, 768], P('tensor')
- grad_out_bias: float32 [2, 768], replicated
- grad_fc_weight: float32 [768, 3072], P(None, 'tensor')
- grad_fc_bias: float32 [3072], P('tensor')
- grad_proj_weight: float32 [3072, 768], P('tensor')
- grad_norm_gain: float32 [2, 768], replicated
- grad_norm_shift: float32 [2, 768], replicated
Inputs may be any that keep to these rules, and one draw needn't show every extreme that they name: `lengths`: one sequence has exactly 1024 tokens and one exactly 64. `dealing`: dealt slot j belongs to data group j. `latent_pos`: each slot's 6 positions are consecutive and lie below every sequence's length.
All inputs are finite; a program needn't handle non-finite values.
Results may differ from a plain program's by a relative error of at most 0.012.
The roundings to bfloat16 on the way count: a program that leaves them out, or rounds other values in their place, can miss the bound.
Values may be sent and summed in bfloat16 or wider, within the bound.
No kernel may reach another device: no remote copies, remote signals or barrier semaphores. Data moves between devices by JAX's collectives and lax.ppermute only.
A program may use at most 192 MiB of HBM per device.

v0:
```python
import jax
import jax.numpy as jnp
from jax import lax
from jax.sharding import PartitionSpec as P

HEAD_DIM = 64


masked_score = -1e30


def layer_norm(features, scale_gain, scale_shift):
    row_mean = jnp.mean(features, axis=-1, keepdims=True)
    centred = features - row_mean
    variance = jnp.mean(centred * centred, axis=-1, keepdims=True)
    return centred * lax.rsqrt(variance + 1e-05) * scale_gain + scale_shift


def tanh_gelu(value):
    return jax.nn.gelu(value, approximate=True)


def contract_rows(left_side, right_side):
    return lax.dot_general(
        left_side, right_side, (((0,), (0,)), ((), ())), preferred_element_type=jnp.float32
    )


def contract_cols(left_side, right_side):
    return lax.dot_general(
        left_side, right_side, (((1,), (1,)), ((), ())), preferred_element_type=jnp.float32
    )


def allowed_keys(offset, row_count, seq_span, length):
    query_pos = offset + jnp.arange(row_count, dtype=jnp.int32)
    key_pos = jnp.arange(seq_span, dtype=jnp.int32)
    return (key_pos[None, :] <= query_pos[:, None]) & (key_pos[None, :] < length)


def attend_forward(sequence_item):
    queries, key_heads, value_heads, length = sequence_item
    seq_span = key_heads.shape[0]
    block_rows = min(512, seq_span)
    score_scale = HEAD_DIM ** (-0.5)
    out_blocks = []
    log_sums = []
    for offset in range(0, seq_span, block_rows):
        scores = (
            jnp.einsum(
                "qhe,khe->hqk",
                queries[offset : offset + block_rows],
                key_heads,
                preferred_element_type=jnp.float32,
            )
            * score_scale
        )
        allowed = allowed_keys(offset, block_rows, seq_span, length)
        scores = jnp.where(allowed[None], scores, masked_score)
        row_top = jnp.max(scores, axis=-1, keepdims=True)
        exponent = jnp.exp(scores - row_top)
        row_total = jnp.sum(exponent, axis=-1, keepdims=True)
        weights_low = (exponent / row_total).astype(jnp.bfloat16)
        out_blocks.append(
            jnp.einsum("hqk,khe->qhe", weights_low, value_heads, preferred_element_type=jnp.float32)
        )
        log_sums.append((row_top + jnp.log(row_total))[..., 0])
    return (jnp.concatenate(out_blocks, axis=0), jnp.concatenate(log_sums, axis=1))


def attend_backward(sequence_item):
    queries, key_heads, value_heads, length, grad_heads, log_sums = sequence_item
    seq_span = key_heads.shape[0]
    block_rows = min(512, seq_span)
    score_scale = HEAD_DIM ** (-0.5)
    query_parts = []
    key_total = jnp.zeros(key_heads.shape, jnp.float32)
    value_total = jnp.zeros(value_heads.shape, jnp.float32)
    for offset in range(0, seq_span, block_rows):
        query_block = queries[offset : offset + block_rows]
        grad_block = grad_heads[offset : offset + block_rows]
        scores = (
            jnp.einsum("qhe,khe->hqk", query_block, key_heads, preferred_element_type=jnp.float32)
            * score_scale
        )
        allowed = allowed_keys(offset, block_rows, seq_span, length)
        probabilities = jnp.where(
            allowed[None], jnp.exp(scores - log_sums[:, offset : offset + block_rows, None]), 0.0
        )
        grad_probs = jnp.einsum(
            "qhe,khe->hqk", grad_block, value_heads, preferred_element_type=jnp.float32
        )
        inner_sum = jnp.sum(probabilities * grad_probs, axis=-1, keepdims=True)
        grad_scores = (probabilities * (grad_probs - inner_sum)).astype(jnp.bfloat16)
        query_parts.append(
            jnp.einsum("hqk,khe->qhe", grad_scores, key_heads, preferred_element_type=jnp.float32)
            * score_scale
        )
        key_total = (
            key_total
            + jnp.einsum(
                "hqk,qhe->khe", grad_scores, query_block, preferred_element_type=jnp.float32
            )
            * score_scale
        )
        value_total = value_total + jnp.einsum(
            "hqk,qhe->khe",
            probabilities.astype(jnp.bfloat16),
            grad_block,
            preferred_element_type=jnp.float32,
        )
    grad_queries = jnp.concatenate(query_parts, axis=0).astype(jnp.bfloat16)
    return (grad_queries, key_total.astype(jnp.bfloat16), value_total.astype(jnp.bfloat16))


def body(
    tokens,
    cotangent,
    thoughts,
    latent_pos,
    lengths,
    dealing,
    qkv_weight,
    qv_bias,
    out_weight,
    out_bias,
    fc_weight,
    fc_bias,
    proj_weight,
    norm_gain,
    norm_shift,
):
    seq_here = thoughts.shape[0]
    half_width = tokens.shape[2]
    group_index = lax.axis_index("dp")
    tensor_index = lax.axis_index("tensor")
    dealt_rows, dealt_cot = (
        lax.all_to_all(tokens[dealing], "dp", split_axis=0, concat_axis=1, tiled=True),
        lax.all_to_all(cotangent[dealing], "dp", split_axis=0, concat_axis=1, tiled=True),
    )
    full_rows, full_cot, full_thoughts = (
        lax.all_gather(dealt_rows, "tensor", axis=2, tiled=True),
        lax.all_gather(dealt_cot, "tensor", axis=2, tiled=True),
        lax.all_gather(thoughts, "tensor", axis=2, tiled=True),
    )
    seq_span = full_rows.shape[1]
    model_width = full_rows.shape[2]
    row_count = seq_here * seq_span
    seq_lengths = lax.dynamic_slice_in_dim(lengths[dealing], group_index * seq_here, seq_here)
    positions = jnp.arange(seq_span, dtype=jnp.int32)
    valid_rows = (
        (positions[None, :] < seq_lengths[:, None]).astype(jnp.float32).reshape(row_count, 1)
    )
    latent_hit = positions[None, :, None] == latent_pos[:, None, :]
    placed = jnp.einsum(
        "spn,snd->spd",
        latent_hit.astype(jnp.bfloat16),
        full_thoughts,
        preferred_element_type=jnp.float32,
    )
    input_rows = jnp.where(
        jnp.any(latent_hit, axis=-1)[..., None], placed, full_rows.astype(jnp.float32)
    ).reshape(row_count, model_width)
    normed = layer_norm(input_rows, norm_gain[0], norm_shift[0]).astype(jnp.bfloat16)
    projected = jnp.einsum("rd,cde->cre", normed, qkv_weight, preferred_element_type=jnp.float32)
    queries = (projected[0] + qv_bias[0]).astype(jnp.bfloat16)
    key_rows = projected[1].astype(jnp.bfloat16)
    value_rows = (projected[2] + qv_bias[1]).astype(jnp.bfloat16)
    heads_here = half_width // HEAD_DIM
    shaped = (seq_here, seq_span, heads_here, HEAD_DIM)
    attended, log_sums = lax.map(
        attend_forward,
        (
            queries.reshape(shaped),
            key_rows.reshape(shaped),
            value_rows.reshape(shaped),
            seq_lengths,
        ),
    )
    heads_out = attended.reshape(row_count, half_width).astype(jnp.bfloat16)
    attn_term = lax.psum(
        jnp.dot(heads_out, out_weight, preferred_element_type=jnp.float32), "tensor"
    )
    residual = input_rows + (attn_term + out_bias[0])
    normed_mlp = layer_norm(residual, norm_gain[1], norm_shift[1]).astype(jnp.bfloat16)
    pre_act = jnp.dot(normed_mlp, fc_weight, preferred_element_type=jnp.float32) + fc_bias
    active = tanh_gelu(pre_act).astype(jnp.bfloat16)
    mlp_share = lax.psum_scatter(
        jnp.dot(active, proj_weight, preferred_element_type=jnp.float32).astype(jnp.bfloat16),
        "tensor",
        scatter_dimension=1,
        tiled=True,
    ).astype(jnp.float32)
    residual_share = lax.dynamic_slice_in_dim(residual, tensor_index * half_width, half_width, 1)
    bias_share = lax.dynamic_slice_in_dim(out_bias[1], tensor_index * half_width, half_width)
    block_share = valid_rows * (residual_share + (mlp_share + bias_share))
    grad_out = valid_rows * full_cot.astype(jnp.float32).reshape(row_count, model_width)
    grad_mlp = grad_out.astype(jnp.bfloat16)
    grad_proj = contract_rows(active, grad_mlp)
    grad_bias_mlp = jnp.sum(grad_mlp.astype(jnp.float32), axis=0)
    _, gelu_back = jax.vjp(tanh_gelu, pre_act)
    grad_pre = gelu_back(contract_cols(grad_mlp, proj_weight))[0].astype(jnp.bfloat16)
    grad_fc = contract_rows(normed_mlp, grad_pre)
    grad_bias_fc = jnp.sum(grad_pre.astype(jnp.float32), axis=0)
    grad_normed_mlp = lax.psum(contract_cols(grad_pre, fc_weight), "tensor")
    _, norm_back_mlp = jax.vjp(layer_norm, residual, norm_gain[1], norm_shift[1])
    grad_resid_norm, grad_gain_mlp, grad_shift_mlp = norm_back_mlp(grad_normed_mlp)
    grad_residual = grad_out + grad_resid_norm
    mlp_small = jnp.concatenate([grad_bias_fc, grad_bias_mlp, grad_gain_mlp, grad_shift_mlp])
    fc_flat = grad_fc.reshape(-1)
    proj_flat = grad_proj.reshape(-1)
    grad_attn = grad_residual.astype(jnp.bfloat16)
    grad_out_proj = contract_rows(heads_out, grad_attn)
    grad_bias_attn = jnp.sum(grad_attn.astype(jnp.float32), axis=0)
    grad_heads = contract_cols(grad_attn, out_weight).astype(jnp.bfloat16)
    grad_queries, grad_keys, grad_values = lax.map(
        attend_backward,
        (
            queries.reshape(shaped),
            key_rows.reshape(shaped),
            value_rows.reshape(shaped),
            seq_lengths,
            grad_heads.reshape(shaped),
            log_sums,
        ),
    )
    grad_qkv_rows = jnp.stack(
        [
            grad_queries.reshape(row_count, half_width),
            grad_keys.reshape(row_count, half_width),
            grad_values.reshape(row_count, half_width),
        ]
    )
    grad_qkv = jnp.einsum("rd,cre->cde", normed, grad_qkv_rows, preferred_element_type=jnp.float32)
    grad_bias_qv = jnp.stack(
        [
            jnp.sum(grad_qkv_rows[0].astype(jnp.float32), axis=0),
            jnp.sum(grad_qkv_rows[2].astype(jnp.float32), axis=0),
        ]
    )
    grad_normed = lax.psum(
        jnp.einsum("cre,cde->rd", grad_qkv_rows, qkv_weight, preferred_element_type=jnp.float32),
        "tensor",
    )
    _, norm_back_attn = jax.vjp(layer_norm, input_rows, norm_gain[0], norm_shift[0])
    grad_rows_norm, grad_gain_attn, grad_shift_attn = norm_back_attn(grad_normed)
    grad_input = grad_residual + grad_rows_norm
    input_share = lax.dynamic_slice_in_dim(grad_input, tensor_index * half_width, half_width, 1)
    attn_small = jnp.concatenate(
        [grad_bias_qv.reshape(-1), grad_bias_attn, grad_gain_attn, grad_shift_attn]
    )
    qkv_flat = grad_qkv.reshape(-1)
    outw_flat = grad_out_proj.reshape(-1)
    block_back, input_back = (
        lax.all_to_all(
            block_share.reshape(seq_here, seq_span, half_width),
            "dp",
            split_axis=1,
            concat_axis=0,
            tiled=True,
        ),
        lax.all_to_all(
            input_share.reshape(seq_here, seq_span, half_width),
            "dp",
            split_axis=1,
            concat_axis=0,
            tiled=True,
        ),
    )
    restore = jnp.zeros_like(dealing).at[dealing].set(jnp.arange(dealing.shape[0], dtype=jnp.int32))
    block_out = block_back[restore]
    input_grad = input_back[restore]
    summed = (
        lax.psum_scatter(fc_flat, "dp", scatter_dimension=0, tiled=True),
        lax.psum_scatter(proj_flat, "dp", scatter_dimension=0, tiled=True),
        lax.psum_scatter(mlp_small, "dp", scatter_dimension=0, tiled=True),
        lax.psum_scatter(qkv_flat, "dp", scatter_dimension=0, tiled=True),
        lax.psum_scatter(outw_flat, "dp", scatter_dimension=0, tiled=True),
        lax.psum_scatter(attn_small, "dp", scatter_dimension=0, tiled=True),
    )
    gathered = (
        lax.all_gather(summed[0], "dp", axis=0, tiled=True),
        lax.all_gather(summed[1], "dp", axis=0, tiled=True),
        lax.all_gather(summed[2], "dp", axis=0, tiled=True),
        lax.all_gather(summed[3], "dp", axis=0, tiled=True),
        lax.all_gather(summed[4], "dp", axis=0, tiled=True),
        lax.all_gather(summed[5], "dp", axis=0, tiled=True),
    )
    hidden_here = fc_bias.shape[0]
    small_mlp = gathered[2]
    grad_fc_bias = small_mlp[:hidden_here]
    bias_mlp = small_mlp[hidden_here : hidden_here + model_width]
    gain_mlp = small_mlp[hidden_here + model_width : hidden_here + 2 * model_width]
    shift_mlp = small_mlp[hidden_here + 2 * model_width :]
    bias_count = 2 * half_width
    small_attn = gathered[5]
    grad_qv_bias = small_attn[:bias_count].reshape(2, half_width)
    bias_attn = small_attn[bias_count : bias_count + model_width]
    gain_attn = small_attn[bias_count + model_width : bias_count + 2 * model_width]
    shift_attn = small_attn[bias_count + 2 * model_width :]
    grad_fc_weight = gathered[0].reshape(fc_weight.shape)
    grad_proj_weight = gathered[1].reshape(proj_weight.shape)
    grad_qkv_weight = gathered[3].reshape(qkv_weight.shape)
    grad_out_weight = gathered[4].reshape(out_weight.shape)
    grad_out_bias = jnp.stack([bias_attn, bias_mlp])
    grad_norm_gain = jnp.stack([gain_attn, gain_mlp])
    grad_norm_shift = jnp.stack([shift_attn, shift_mlp])
    return (
        block_out,
        input_grad,
        grad_qkv_weight,
        grad_qv_bias,
        grad_out_weight,
        grad_out_bias,
        grad_fc_weight,
        grad_fc_bias,
        grad_proj_weight,
        grad_norm_gain,
        grad_norm_shift,
    )


def solution(mesh):
    return jax.shard_map(
        body,
        mesh=mesh,
        in_specs=(
            P(None, "dp", "tensor"),
            P(None, "dp", "tensor"),
            P("dp", None, "tensor"),
            P("dp", None),
            P(),
            P(),
            P(None, None, "tensor"),
            P(None, "tensor"),
            P("tensor", None),
            P(),
            P(None, "tensor"),
            P("tensor"),
            P("tensor", None),
            P(),
            P(),
        ),
        out_specs=(
            P(None, "dp", "tensor"),
            P(None, "dp", "tensor"),
            P(None, None, "tensor"),
            P(None, "tensor"),
            P("tensor", None),
            P(),
            P(None, "tensor"),
            P("tensor"),
            P("tensor", None),
            P(),
            P(),
        ),
        check_vma=False,
    )
```

profile of v0, /device:TPU:0, one launch (start us, length us, event | category | flops | bytes accessed | tf_op | source)
XLA Modules:
  0.0 1021.8 jit_solution(2742351826906348683)
XLA Ops:
  10.8 27.5 %all_to_all.48 = bf16[16,64,384]{2,1,0:T(8,128)(2,1)S(1)} all-to-all(bf16[16,64,384]{2,1,0:T(8,128)(2,1)} %gather_fusion.1), channel_id=1, replica_groups=mesh['dp'=16,'tensor'=2] {'dp'}, dimensions={0} | all-to-all | bytes 1572864 | tf_op jit(solution)/shard_map/all_to_all | solution.py:138
  40.9 4.4 all_gather.27
  47.7 18.5 %all-gather.7.cloned.1.call-done = bf16[1,1024,768]{1,2,0:T(8,128)(2,1)} async-done(((bf16[1,1024,384]{1,2,0:T(8,128)(2,1)}), bf16[1,1024,768]{1,2,0:T(8,128)(2,1)}) %all-gather.7.cloned.1.call-update) | async-done | bytes 1572880 | tf_op jit(solution)/shard_map/all_gather | solution.py:142
  75.8 3.8 fusion
  80.3 4.3 fusion.33
  87.1 3.6 fusion.1
  91.8 4.3 fusion.34
  102.5 5.7 all-to-all-start.2
  110.3 16.7 %all-to-all-done.2 = bf16[16,64,384]{2,1,0:T(8,128)(2,1)} async-done(((bf16[16,64,384]{2,1,0:T(8,128)(2,1)}), bf16[16,64,384]{2,1,0:T(8,128)(2,1)}, u32[]{:S(2)}, u32[]{:S(2)}) %all-to-all-start.2) | async-done | bytes 786464 | tf_op jit(solution)/shard_map/all_to_all | solution.py:139
  129.3 56.5 %all-reduce.16.cloned.1.call-done = f32[1024,768]{0,1:T(8,128)} async-done(((f32[1024,768]{0,1:T(8,128)}), f32[1024,768]{0,1:T(8,128)}) %all-reduce.16.cloned.1.call-update) | async-done | bytes 3145744 | tf_op jit(solution)/shard_map/psum | solution.py:181
  185.8 3.3 fusion.71
  191.9 5.2 fusion.68
  197.1 18.0 %all-gather.9.cloned.1.call-done = bf16[1,1024,768]{1,2,0:T(8,128)(2,1)} async-done(((bf16[1,1024,384]{1,2,0:T(8,128)(2,1)}), bf16[1,1024,768]{1,2,0:T(8,128)(2,1)}) %all-gather.9.cloned.1.call-update) | async-done | bytes 1572880 | tf_op jit(solution)/shard_map/all_gather | solution.py:143
  215.2 9.5 convert_reduce_fusion
  226.4 4.3 fusion.80
  232.8 9.9 fusion.35
  242.8 5.9 reshape.434
  248.6 7.8 fusion.67
  256.4 5.7 reshape.432
  262.1 54.6 %all-reduce.18.cloned.1.call-done = f32[1024,768]{0,1:T(8,128)} async-done(((f32[1024,768]{0,1:T(8,128)}), f32[1024,768]{0,1:T(8,128)}) %all-reduce.18.cloned.1.call-update) | async-done | bytes 3145744 | tf_op jit(solution)/shard_map/psum | solution.py:205
  316.7 3.5 multiply_reduce_fusion.5
  328.7 7.4 fusion.11
  336.2 10.2 multiply_reduce_fusion
  346.4 7.5 multiply_reduce_fusion.1
  353.9 17.8 %multiply_convert_fusion = (bf16[6,512,1024]{2,1,0:T(8,128)(2,1)}, bf16[6,512,1024]{2,1,0:T(8,128)(2,1)}) fusion(f32[6,512,1024]{2,1,0:T(8,128)} %get-tuple-element.115, f32[6,512,1024]{2,1,0:T(8,128)} %copy-done.3, f32[6,512]{1,0:T(8,128)S(1)} %get-tuple-element.114, f32[6,512]{1,0:T(8,128)S(1)} %copy-done.32, pred[512,1024]{1,0:T(8,128)(4,1)S(1)} %copy-done.15, ...), kind=kLoop, calls=%fused_computation.6 | loop fusion | flops 37748736 | bytes 64012288 | tf_op jit(solution)/shard_map/while/body/eval_jaxpr/convert_element_type | solution.py:94
  371.8 5.7 fusion.29
  382.6 9.5 convert_reduce_fusion.3
  394.4 5.7 fusion.30
  400.1 4.0 multiply_convert_fusion.3
  407.8 6.6 convolution_bitcast_fusion.1
  414.4 5.2 copy.108
  419.6 4.5 reshape.427
  424.2 7.2 convolution_convert_fusion
  431.6 5.7 convolution_bitcast_fusion.2
  439.3 241.1 %all-reduce.22.cloned.1.call-done = (f32[884736]{0:T(1024)}, f32[294912]{0:T(1024)}, f32[1179648]{0:T(1024)}, f32[1179648]{0:T(1024)}) async-done(((f32[884736]{0:T(1024)}, f32[294912]{0:T(1024)}, f32[1179648]{0:T(1024)}, f32[1179648]{0:T(1024)}), (f32[884736]{0:T(1024)}, f32[294912]{0:T(1024)}, f32[1179648]{0:T(1024)}, f32[1179648]{0:T(1024)})) %all-reduce.22.cloned.1.call-update) | async-done | bytes 14155792
  688.5 20.8 %reduce-scatter.2.cloned.1.call-done = bf16[1024,384]{0,1:T(8,128)(2,1)} async-done(((bf16[1024,768]{0,1:T(8,128)(2,1)}), bf16[1024,384]{0,1:T(8,128)(2,1)}) %reduce-scatter.2.cloned.1.call-update) | async-done | bytes 786448 | tf_op jit(solution)/shard_map/reduce_scatter | solution.py:188
  712.4 4.8 copy.96
  717.2 5.7 all-to-all-start.1
  722.9 75.2 %all-reduce.20.cloned.1.call-done = f32[1024,768]{0,1:T(8,128)} async-done(((f32[1024,768]{0,1:T(8,128)}), f32[1024,768]{0,1:T(8,128)}) %all-reduce.20.cloned.1.call-update) | async-done | bytes 3145744 | tf_op jit(solution)/shard_map/psum | solution.py:241
  798.1 4.0 multiply_reduce_fusion.3
  806.1 4.9 copy.105
  811.0 5.7 all-to-all-start.3
  826.2 78.8 %all-reduce.9 = (f32[3072]{0:T(1024)S(1)}, f32[3840]{0:T(1024)S(1)}) all-reduce(f32[3072]{0:T(1024)S(1)} %pad_maximum_fusion.5, f32[3840]{0:T(1024)S(1)} %pad_maximum_fusion.4), channel_id=4, replica_groups=mesh['dp'=16,'tensor'=2] {'dp'}, use_global_device_ids=true, to_apply=%region_26.27.clone | all-reduce | flops 6912 | bytes 55296
  905.4 59.4 %all-reduce.8 = (f32[3072]{0:T(1024)S(1)}, f32[3840]{0:T(1024)S(1)}) all-reduce(f32[3072]{0:T(1024)S(1)} %dynamic-slice_dynamic-update-slice_fusion.1, f32[3840]{0:T(1024)S(1)} %dynamic-slice_dynamic-update-slice_fusion), channel_id=1, replica_groups=mesh['dp'=16,'tensor'=2] {'dp'}, use_global_device_ids=true, to_apply=%add | all-reduce | flops 6912 | bytes 55296
  976.1 4.8 reshape.428
  980.9 6.1 reshape.435
  987.0 22.3 %all-gather.15.cloned.1.call-done = f32[1179648]{0:T(1024)} async-done(((f32[73728]{0:T(1024)}), f32[1179648]{0:T(1024)}) %all-gather.15.cloned.1.call-update) | async-done | bytes 4718608 | tf_op jit(solution)/shard_map/all_gather | solution.py:282
  1009.3 5.8 reshape.433
  (282 shorter events, 92.9 us)
Async XLA Ops:
  7.2 208.0 %copy-start = (bf16[1536,768]{1,0:T(8,128)(2,1)S(1)}, bf16[1536,768]{1,0:T(8,128)(2,1)}, u32[]{:S(2)}) copy-start(bf16[1536,768]{1,0:T(8,128)(2,1)} %param.27) | copy-start | bytes 7077892
  7.2 32.4 %copy-start.1 = (s32[16]{0:T(128)S(1)}, s32[16]{0:T(128)}, u32[]{:S(2)}) copy-start(s32[16]{0:T(128)} %param.19) | copy-start | bytes 196
  7.2 33.0 %copy-start.69 = (f32[2,384]{1,0:T(2,128)S(1)}, f32[2,384]{1,0:T(2,128)}, u32[]{:S(2)}) copy-start(f32[2,384]{1,0:T(2,128)} %param.22) | copy-start | bytes 9220
  7.2 33.7 %copy-start.64 = (bf16[1,6,384]{2,1,0:T(8,128)(2,1)S(1)}, bf16[1,6,384]{2,1,0:T(8,128)(2,1)}, u32[]{:S(2)}) copy-start(bf16[1,6,384]{2,1,0:T(8,128)(2,1)} %param.17) | copy-start | bytes 13828
  7.2 38.8 %copy-start.62 = (f32[2,768]{1,0:T(2,128)S(1)}, f32[2,768]{1,0:T(2,128)}, u32[]{:S(2)}) copy-start(f32[2,768]{1,0:T(2,128)} %param.28) | copy-start | bytes 18436
  7.2 38.8 %copy-start.63 = (f32[2,768]{1,0:T(2,128)S(1)}, f32[2,768]{1,0:T(2,128)}, u32[]{:S(2)}) copy-start(f32[2,768]{1,0:T(2,128)} %param.29) | copy-start | bytes 18436
  7.2 38.9 %copy-start.71 = (s32[1,6]{1,0:T(1,128)S(1)}, s32[1,6]{1,0:T(1,128)}, u32[]{:S(2)}) copy-start(s32[1,6]{1,0:T(1,128)} %param.18) | copy-start | bytes 76
  7.3 58.9 %all-gather.7.cloned.1.call-start = ((), (), s32[]{:S(2)}) async-start(), calls=%async_computation.5 | async-start | bytes 2359296 | tf_op jit(solution)/shard_map/all_gather | solution.py:142
  8.1 39.6 %copy-start.72 = (s32[16]{0:T(128)}, s32[16]{0:T(128)S(1)}, u32[]{:S(2)}) copy-start(s32[16]{0:T(128)S(1)} %compare_select_fusion.1) | copy-start | bytes 196
  39.5 146.3 %all-reduce.16.cloned.1.call-start = ((), (), s32[]{:S(2)}) async-start(), calls=%async_computation.6 | async-start | bytes 6291456 | tf_op jit(solution)/shard_map/psum | solution.py:181
  46.1 22.8 %copy-start.43 = (f32[768]{0:T(1024)}, f32[768]{0:T(1024)S(1)}, u32[]{:S(2)}) copy-start(f32[768]{0:T(1024)S(1)} %get-tuple-element.69) | copy-start | bytes 9220
  46.1 144.1 %copy-start.41 = (f32[768]{0:T(1024)}, f32[768]{0:T(1024)S(1)}, u32[]{:S(2)}) copy-start(f32[768]{0:T(1024)S(1)} %get-tuple-element.68) | copy-start | bytes 9220
  46.1 22.7 %copy-start.65 = (f32[768]{0:T(1024)}, f32[768]{0:T(1024)S(1)}, u32[]{:S(2)}) copy-start(f32[768]{0:T(1024)S(1)} %get-tuple-element.71) | copy-start | bytes 9220
  46.1 144.0 %copy-start.67 = (f32[768]{0:T(1024)}, f32[768]{0:T(1024)S(1)}, u32[]{:S(2)}) copy-start(f32[768]{0:T(1024)S(1)} %get-tuple-element.70) | copy-start | bytes 9220
  72.8 17.9 %copy-start.20 = (bf16[1024,6,64]{0,2,1:T(8,128)(2,1)}, bf16[1024,6,64]{0,2,1:T(8,128)(2,1)S(1)}, u32[]{:S(2)}) copy-start(bf16[1024,6,64]{0,2,1:T(8,128)(2,1)S(1)} %add_convert_fusion.3) | copy-start | bytes 2359300
  102.5 24.4 %all-to-all-start.2 = ((bf16[16,64,384]{2,1,0:T(8,128)(2,1)}), bf16[16,64,384]{2,1,0:T(8,128)(2,1)}, u32[]{:S(2)}, u32[]{:S(2)}) async-start(bf16[16,64,384]{2,1,0:T(8,128)(2,1)} %gather_fusion.3), calls=%async_computation.3 | async-start | bytes 1572864 | tf_op jit(solution)/shard_map/all_to_all | solution.py:139
  108.2 107.0 %all-gather.9.cloned.1.call-start = ((), (), s32[]{:S(2)}) async-start(), calls=%async_computation.8 | async-start | bytes 2359296 | tf_op jit(solution)/shard_map/all_gather | solution.py:143
  108.9 106.3 %copy-start.47 = (f32[1024]{0:T(1024)}, f32[1024]{0:T(1024)S(1)}, u32[]{:S(2)}) copy-start(f32[1024]{0:T(1024)S(1)} %fusion.50) | copy-start | bytes 12292
  129.2 187.5 %all-reduce.18.cloned.1.call-start = ((), (), s32[]{:S(2)}) async-start(), calls=%async_computation.9 | async-start | bytes 6291456 | tf_op jit(solution)/shard_map/psum | solution.py:205
  215.2 11.2 %copy-start.74 = (bf16[768,1536]{1,0:T(8,128)(2,1)S(1)}, bf16[768,1536]{1,0:T(8,128)(2,1)}, u32[]{:S(2)}) copy-start(bf16[768,1536]{1,0:T(8,128)(2,1)} %param.25) | copy-start | bytes 7077892
  230.7 449.7 %all-reduce.22.cloned.1.call-start = ((), (), s32[]{:S(2)}) async-start(), calls=%async_computation.15 | async-start | bytes 28311552
  328.6 17.8 %copy-start.29 = (bf16[512,384]{0,1:T(8,128)(2,1)}, bf16[512,384]{0,1:T(8,128)(2,1)S(1)}, u32[]{:S(2)}) copy-start(bf16[512,384]{0,1:T(8,128)(2,1)S(1)} %get-tuple-element.89) | copy-start | bytes 1179652
  328.7 7.4 copy-start.21
  328.7 17.6 %slice-start = ((s8[12582912]{0:T(1024)(128)(4,1)}), s8[4194304]{0:T(1024)(128)(4,1)S(1)}, s32[]{:S(2)}) async-start(s8[12582912]{0:T(1024)(128)(4,1)} %bitcast.135), calls=%async_computation.16 | async-start | bytes 8388608
  328.7 17.6 %slice-start.1 = ((s8[12582912]{0:T(1024)(128)(4,1)}), s8[4194304]{0:T(1024)(128)(4,1)S(1)}, s32[]{:S(2)}) async-start(s8[12582912]{0:T(1024)(128)(4,1)} %bitcast.135), calls=%async_computation.17 | async-start | bytes 8388608
  336.2 10.2 %slice-start.2 = ((s8[12582912]{0:T(1024)(128)(4,1)}), s8[4194304]{0:T(1024)(128)(4,1)S(1)}, s32[]{:S(2)}) async-start(s8[12582912]{0:T(1024)(128)(4,1)} %bitcast.135), calls=%async_computation.18 | async-start | bytes 8388608
  336.2 10.2 %copy-start.13 = (pred[512,1024]{1,0:T(8,128)(4,1)S(1)}, pred[512,1024]{1,0:T(8,128)(4,1)}, u32[]{:S(2)}) copy-start(pred[512,1024]{1,0:T(8,128)(4,1)} %get-tuple-element.102) | copy-start | bytes 1572868
  407.8 6.6 copy-start.31
  424.1 7.5 copy-start.30
  424.1 285.2 %reduce-scatter.2.cloned.1.call-start = ((), (), s32[]{:S(2)}) async-start(), calls=%async_computation.7 | async-start | bytes 2359296 | tf_op jit(solution)/shard_map/reduce_scatter | solution.py:188
  431.4 366.7 %all-reduce.20.cloned.1.call-start = ((), (), s32[]{:S(2)}) async-start(), calls=%async_computation.10 | async-start | bytes 6291456 | tf_op jit(solution)/shard_map/psum | solution.py:241
  437.3 251.2 %copy-start.61 = (f32[1,768]{1,0:T(1,128)S(1)}, f32[1,768]{1,0:T(1,128)}, u32[]{:S(2)}) copy-start(f32[1,768]{1,0:T(1,128)} %get-tuple-element.100) | copy-start | bytes 9220
  437.3 272.0 %copy-start.49 = (f32[1024]{0:T(1024)S(1)}, f32[1024]{0:T(1024)}, u32[]{:S(2)}) copy-start(f32[1024]{0:T(1024)} %copy-done.47) | copy-start | bytes 12292
  437.4 536.3 %all-gather.13.cloned.1.call-start = ((), (), s32[]{:S(2)}) async-start(), calls=%async_computation.12 | async-start | bytes 1253376 | tf_op jit(solution)/shard_map/all_gather | solution.py:286
  682.0 294.2 %all-gather.11.cloned.1.call-start = ((), (), s32[]{:S(2)}) async-start(), calls=%async_computation.11 | async-start | bytes 3760128 | tf_op jit(solution)/shard_map/all_gather | solution.py:285
  684.3 296.6 %all-gather.17.cloned.1.call-start = ((), (), s32[]{:S(2)}) async-start(), calls=%async_computation.14 | async-start | bytes 5013504 | tf_op jit(solution)/shard_map/all_gather | solution.py:283
  686.7 322.6 %all-gather.15.cloned.1.call-start = ((), (), s32[]{:S(2)}) async-start(), calls=%async_computation.13 | async-start | bytes 5013504 | tf_op jit(solution)/shard_map/all_gather | solution.py:282
  717.2 93.8 %all-to-all-start.1 = ((f32[1,1024,384]{2,0,1:T(1,128)}), f32[1,1024,384]{2,0,1:T(1,128)}, u32[]{:S(2)}, u32[]{:S(2)}) async-start(f32[1,1024,384]{2,0,1:T(1,128)} %copy.96), calls=%async_computation.2 | async-start | bytes 3145728 | tf_op jit(solution)/shard_map/all_to_all | solution.py:255
  722.9 79.2 %copy-start.51 = (f32[1024]{0:T(1024)S(1)}, f32[1024]{0:T(1024)}, u32[]{:S(2)}) copy-start(f32[1024]{0:T(1024)} %copy-done.50) | copy-start | bytes 12292
  806.1 13.9 %copy-start.68 = (f32[6,64]{1,0:T(8,128)S(1)}, f32[6,64]{1,0:T(8,128)}, u32[]{:S(2)}) copy-start(f32[6,64]{1,0:T(8,128)} %get-tuple-element.116) | copy-start | bytes 4612
  806.1 14.0 %copy-start.24 = (bf16[6,64,512]{2,1,0:T(8,128)(2,1)S(1)}, bf16[6,64,512]{2,1,0:T(8,128)(2,1)}, u32[]{:S(2)}) copy-start(bf16[6,64,512]{2,1,0:T(8,128)(2,1)} %fusion.29) | copy-start | bytes 1179652
  806.1 14.0 %copy-start.25 = (bf16[6,64,512]{2,1,0:T(8,128)(2,1)S(1)}, bf16[6,64,512]{2,1,0:T(8,128)(2,1)}, u32[]{:S(2)}) copy-start(bf16[6,64,512]{2,1,0:T(8,128)(2,1)} %fusion.30) | copy-start | bytes 1179652
  806.1 14.2 %copy-start.57 = (f32[768]{0:T(1024)S(1)}, f32[768]{0:T(1024)}, u32[]{:S(2)}) copy-start(f32[768]{0:T(1024)} %get-tuple-element.88) | copy-start | bytes 9220
  806.1 14.2 %copy-start.58 = (f32[768]{0:T(1024)S(1)}, f32[768]{0:T(1024)}, u32[]{:S(2)}) copy-start(f32[768]{0:T(1024)} %get-tuple-element.52) | copy-start | bytes 9220
  806.1 14.2 %copy-start.59 = (f32[768]{0:T(1024)S(1)}, f32[768]{0:T(1024)}, u32[]{:S(2)}) copy-start(f32[768]{0:T(1024)} %get-tuple-element.56) | copy-start | bytes 9220
  806.1 14.2 %copy-start.60 = (f32[1536]{0:T(1024)S(1)}, f32[1536]{0:T(1024)}, u32[]{:S(2)}) copy-start(f32[1536]{0:T(1024)} %get-tuple-element.118) | copy-start | bytes 18436
  811.0 156.8 %all-to-all-start.3 = ((f32[1,1024,384]{2,0,1:T(1,128)}), f32[1,1024,384]{2,0,1:T(1,128)}, u32[]{:S(2)}, u32[]{:S(2)}) async-start(f32[1,1024,384]{2,0,1:T(1,128)} %copy.105), calls=%async_computation.4 | async-start | bytes 3145728 | tf_op jit(solution)/shard_map/all_to_all | solution.py:262
  820.4 5.9 copy-start.56
  (46 other events, 146.2 us)
Sparse Core Ops, SparseCore 0:
  39.6 26.4 all-gather.6
  100.0 85.8 all-reduce.15
  187.9 27.1 all-gather.8
  230.8 85.8 all-reduce.17
  424.2 256.1 all-reduce.21
  683.1 26.1 reduce-scatter.1
  712.2 85.8 all-reduce.19
  800.9 49.1 all-gather.12
  852.3 47.8 all-gather.10
  902.4 52.2 all-gather.16
  957.6 51.6 all-gather.14
where the time goes:
time: 1030 us; the launch traced here: 1020 us
  waiting for transfers between devices  524 us (51%)
  blocking collectives  170 us (17%)
  matrix products  132 us (13%)
  local copies, waits for them, and re-layouts  104 us (10%)
  other arithmetic  54.6 us (5%)
  between operations  19.5 us (2%)
  starting transfers between devices  17.6 us (2%)
    unnamed x12, waiting for transfers between devices  241 us
    unnamed x2, blocking collectives  138 us
    psum x1, waiting for transfers between devices, body(): lax.psum(jnp.einsum('cre,cde->rd', grad_qkv_rows, qkv_weight, preferred_e...  75.2 us
    psum x1, waiting for transfers between devices, body(): lax.psum(jnp.dot(heads_out, out_weight, preferred_element_type=jnp.float3...  56.5 us
    psum x1, waiting for transfers between devices, body(): grad_normed_mlp = lax.psum(contract_cols(grad_pre, fc_weight), 'tensor')  54.6 us
    all_to_all x1, blocking collectives, body(): lax.all_to_all(tokens[dealing], 'dp', split_axis=0, concat_axis=1, tiled=...  27.5 us
    unnamed x171, local copies, waits for them, and re-layouts  24.9 us
    all_gather x1, waiting for transfers between devices, body(): lax.all_gather(summed[0], 'dp', axis=0, tiled=True)  22.3 us
  transfers between devices with their start and end apart: 14, of which 9 were waited for; matrix products, arithmetic and copies ran while one was open for 12% of the time, Pallas kernels for 0%

commit v1 on v0

v1 whole, which is shorter than its diff:
```python
import functools

import jax
import jax.numpy as jnp
from jax import lax
from jax.experimental import pallas as pl
from jax.experimental.pallas import tpu as pltpu
from jax.sharding import PartitionSpec as P

HEAD_DIM = 64
LANES = 128
AXES = ("dp", "tensor")
SCALE = HEAD_DIM ** (-0.5)
MASKED = -1e30
BF16 = jnp.bfloat16
F32 = jnp.float32


def dot_nn(left, right):
    return lax.dot_general(left, right, (((1,), (0,)), ((), ())), preferred_element_type=F32)


def dot_nt(left, right):
    return lax.dot_general(left, right, (((1,), (1,)), ((), ())), preferred_element_type=F32)


def dot_tn(left, right):
    return lax.dot_general(left, right, (((0,), (0,)), ((), ())), preferred_element_type=F32)


def own_mask(tile, start, core, length, block):
    key = lax.broadcasted_iota(jnp.int32, (tile, tile), 0)
    query = lax.broadcasted_iota(jnp.int32, (tile, tile), 1)
    key_row = start + key
    key_pos = (2 * (key_row // block) + core) * block + key_row % block
    return (key <= query) & (key_pos < length)


def other_mask(tile, start, core, length, block):
    key = lax.broadcasted_iota(jnp.int32, (tile, tile), 0)
    query = lax.broadcasted_iota(jnp.int32, (tile, tile), 1)
    key_row = start + key
    key_pos = (2 * (key_row // block) + 1 - core) * block + key_row % block
    return (key // block <= query // block - (1 - core)) & (key_pos < length)


def attend_forward_kernel(tile, block, info, q_ref, ko_ref, vo_ref, kx_ref, vx_ref, out_ref, lse_ref):
    core, length = info[0], info[1]
    rows = q_ref.shape[0]
    lane = lax.broadcasted_iota(jnp.int32, (1, LANES), 1)
    vo_t = vo_ref[...].T
    vx_t = vx_ref[...].T
    for start in range(0, rows, tile):
        stop = start + tile
        mask_own = own_mask(tile, start, core, length, block)
        mask_other = other_mask(tile, start, core, length, block)
        query = q_ref[start:stop, :] * jnp.asarray(SCALE, BF16)
        outs = []
        for half in range(2):
            picked = jnp.where(lane // HEAD_DIM == half, query, jnp.zeros_like(query))
            s_own = dot_nt(ko_ref[:stop, :], picked)
            s_other = dot_nt(kx_ref[:stop, :], picked)
            d_own = jnp.where(mask_own, s_own[start:], MASKED)
            d_other = jnp.where(mask_other, s_other[start:], MASKED)
            if start:
                s_own = jnp.concatenate([s_own[:start], d_own], axis=0)
                s_other = jnp.concatenate([s_other[:start], d_other], axis=0)
            else:
                s_own, s_other = d_own, d_other
            top = jnp.maximum(
                jnp.max(s_own, axis=0, keepdims=True), jnp.max(s_other, axis=0, keepdims=True)
            )
            e_own = jnp.exp(s_own - top)
            e_other = jnp.exp(s_other - top)
            total = jnp.sum(e_own, axis=0, keepdims=True) + jnp.sum(e_other, axis=0, keepdims=True)
            lanes = slice(half * HEAD_DIM, (half + 1) * HEAD_DIM)
            mixed = dot_nn(vo_t[lanes, :stop], e_own.astype(BF16)) + dot_nn(
                vx_t[lanes, :stop], e_other.astype(BF16)
            )
            outs.append(mixed / total)
            lse_ref[0, half : half + 1, start:stop] = top + jnp.log(total)
        out_ref[start:stop, :] = jnp.concatenate(outs, axis=0).T.astype(BF16)


def attend_backward_kernel(
    tile, block, info, q_ref, ko_ref, vo_ref, kx_ref, vx_ref, go_ref, out_ref, lse_ref,
    dq_ref, dko_ref, dvo_ref, dkx_ref, dvx_ref, ako, avo, akx, avx,
):
    core, length = info[0], info[1]
    rows = q_ref.shape[0]
    lane = lax.broadcasted_iota(jnp.int32, (1, LANES), 1)
    ko_t = ko_ref[...].T
    kx_t = kx_ref[...].T
    for acc in (ako, avo, akx, avx):
        acc[...] = jnp.zeros_like(acc)
    for start in range(0, rows, tile):
        stop = start + tile
        mask_own = own_mask(tile, start, core, length, block)
        mask_other = other_mask(tile, start, core, length, block)
        query = q_ref[start:stop, :] * jnp.asarray(SCALE, BF16)
        grad = go_ref[start:stop, :]
        product = grad.astype(F32) * out_ref[start:stop, :].astype(F32)
        parts = []
        for half in range(2):
            mine = lane // HEAD_DIM == half
            picked = jnp.where(mine, query, jnp.zeros_like(query))
            grad_half = jnp.where(mine, grad, jnp.zeros_like(grad))
            pick = jnp.broadcast_to(jnp.where(mine, 1.0, 0.0).astype(F32), (8, LANES))
            inner = lax.dot_general(
                pick, product, (((1,), (1,)), ((), ())),
                precision=lax.Precision.HIGHEST, preferred_element_type=F32,
            )[:1]
            lse = lse_ref[0, half : half + 1, start:stop]
            lanes = slice(half * HEAD_DIM, (half + 1) * HEAD_DIM)
            part = jnp.zeros((HEAD_DIM, tile), F32)
            for key_ref, value_ref, key_t, mask, acc_k, acc_v in (
                (ko_ref, vo_ref, ko_t, mask_own, ako, avo),
                (kx_ref, vx_ref, kx_t, mask_other, akx, avx),
            ):
                prob = jnp.exp(dot_nt(key_ref[:stop, :], picked) - lse)
                last = jnp.where(mask, prob[start:], 0.0)
                prob = jnp.concatenate([prob[:start], last], axis=0) if start else last
                grad_prob = dot_nt(value_ref[:stop, :], grad_half)
                grad_score = (prob * (grad_prob - inner)).astype(BF16)
                acc_v[:stop, :] += dot_nn(prob.astype(BF16), grad_half)
                acc_k[:stop, :] += dot_nn(grad_score, picked)
                part = part + dot_nn(key_t[lanes, :stop], grad_score)
            parts.append(part)
        dq_ref[start:stop, :] = (jnp.concatenate(parts, axis=0) * SCALE).T.astype(BF16)
    for acc, ref in ((ako, dko_ref), (avo, dvo_ref), (akx, dkx_ref), (avx, dvx_ref)):
        ref[...] = acc[...].astype(ref.dtype)


def attend_forward(info, block, queries, keys_own, values_own, keys_other, values_other):
    rows, width = queries.shape
    pairs = width // LANES
    tile = min(256, rows)
    column = pl.BlockSpec((rows, LANES), lambda pair, info: (0, pair))
    return pl.pallas_call(
        functools.partial(attend_forward_kernel, tile, block),
        grid_spec=pltpu.PrefetchScalarGridSpec(
            num_scalar_prefetch=1,
            grid=(pairs,),
            in_specs=[column] * 5,
            out_specs=[column, pl.BlockSpec((1, 2, rows), lambda pair, info: (pair, 0, 0))],
        ),
        out_shape=[
            jax.ShapeDtypeStruct((rows, width), BF16),
            jax.ShapeDtypeStruct((pairs, 2, rows), F32),
        ],
        name="attend_forward",
    )(info, queries, keys_own, values_own, keys_other, values_other)


def attend_backward(info, block, queries, keys_own, values_own, keys_other, values_other, grad_heads, heads_out, lse):
    rows, width = queries.shape
    pairs = width // LANES
    tile = min(256, rows)
    column = pl.BlockSpec((rows, LANES), lambda pair, info: (0, pair))
    return pl.pallas_call(
        functools.partial(attend_backward_kernel, tile, block),
        grid_spec=pltpu.PrefetchScalarGridSpec(
            num_scalar_prefetch=1,
            grid=(pairs,),
            in_specs=[column] * 7 + [pl.BlockSpec((1, 2, rows), lambda pair, info: (pair, 0, 0))],
            out_specs=[column] * 5,
            scratch_shapes=[pltpu.VMEM((rows, LANES), F32)] * 4,
        ),
        out_shape=[
            jax.ShapeDtypeStruct((rows, width), BF16),
            jax.ShapeDtypeStruct((rows, width), F32),
            jax.ShapeDtypeStruct((rows, width), F32),
            jax.ShapeDtypeStruct((rows, width), BF16),
            jax.ShapeDtypeStruct((rows, width), BF16),
        ],
        name="attend_backward",
    )(info, queries, keys_own, values_own, keys_other, values_other, grad_heads, heads_out, lse)


def normalize(features):
    mean = jnp.mean(features, axis=-1, keepdims=True)
    centred = features - mean
    variance = jnp.mean(centred * centred, axis=-1, keepdims=True)
    scale = lax.rsqrt(variance + 1e-05)
    return centred * scale, scale


def norm_back(grad, gain, xhat, scale):
    scaled = grad * gain
    row = scale * (
        scaled
        - jnp.mean(scaled, axis=-1, keepdims=True)
        - xhat * jnp.mean(scaled * xhat, axis=-1, keepdims=True)
    )
    return row, jnp.sum(grad * xhat, axis=0), jnp.sum(grad, axis=0)


ROOT = 0.7978845608028654
CUBE = 0.044715


def gelu_and_slope(value):
    square = value * value
    turn = jnp.tanh(ROOT * value * (1.0 + CUBE * square))
    slope = 0.5 * (1.0 + turn) + 0.5 * value * (1.0 - turn * turn) * ROOT * (1.0 + 3.0 * CUBE * square)
    return 0.5 * value * (1.0 + turn), slope


def solution(mesh):
    groups = mesh.shape["dp"]
    bits = groups.bit_length() - 1
    assert groups == 1 << bits and mesh.shape["tensor"] == 2

    def pairs_of(change):
        table = []
        for group in range(groups):
            for side in range(2):
                to_group, to_side = change(group, side)
                table.append((group * 2 + side, to_group * 2 + to_side))
        return table

    tensor_pairs = pairs_of(lambda group, side: (group, 1 - side))
    bit_pairs = [pairs_of(lambda group, side, k=k: (group ^ (1 << k), side)) for k in range(bits)]
    deal_groups = [
        [group * 2 + side for group in range(core, groups, 2) for side in range(2)] for core in range(2)
    ]

    def body(
        tokens, cotangent, thoughts, latent_pos, lengths, dealing, qkv_weight, qv_bias, out_weight,
        out_bias, fc_weight, fc_bias, proj_weight, norm_gain, norm_shift,
    ):
        group = lax.axis_index("dp")
        side = lax.axis_index("tensor")
        core = group % 2
        slot = group - core + side
        slots, block, half_width = tokens.shape
        width = 2 * half_width
        rows = slots * block // 2
        hidden_half = fc_weight.shape[1]

        def cross(value):
            return lax.ppermute(value, AXES, tensor_pairs)

        def flip(value, bit=0):
            return lax.ppermute(value, AXES, bit_pairs[bit])

        def part(value, index):
            size = value.shape[0] // 2
            return lax.dynamic_slice_in_dim(value, index * size, size, 0)

        def join(flag, mine, theirs, axis=0):
            return jnp.where(
                flag == 0,
                jnp.concatenate([mine, theirs], axis=axis),
                jnp.concatenate([theirs, mine], axis=axis),
            )

        def fetch(weight):
            direct = cross(part(weight, core))
            return join(core, direct, flip(direct))

        def deal(array):
            pieces = lax.all_to_all(
                array[dealing], AXES, split_axis=0, concat_axis=0, tiled=True, axis_index_groups=deal_groups
            )
            pieces = pieces.reshape(slots // 2, 2, block, half_width)
            return pieces.transpose(0, 2, 1, 3).reshape(rows, width)

        restore = jnp.zeros_like(dealing).at[dealing].set(jnp.arange(slots, dtype=jnp.int32))

        def undeal(array):
            pieces = array.astype(BF16).reshape(slots // 2, block, 2, half_width).transpose(0, 2, 1, 3)
            pieces = lax.all_to_all(
                pieces.reshape(slots, block, half_width), AXES, split_axis=0, concat_axis=0, tiled=True,
                axis_index_groups=deal_groups,
            )
            return pieces[restore].astype(F32)

        dealt = deal(tokens)
        qkv_flat = qkv_weight.reshape(3 * width, half_width)
        qkv_other = fetch(qkv_flat).reshape(3, width, half_width)
        out_other = fetch(out_weight)
        fc_other = fetch(fc_weight)
        proj_other = fetch(proj_weight)
        biases_other = cross(jnp.concatenate([qv_bias.reshape(-1), fc_bias]))
        qv_other = biases_other[:width].reshape(2, half_width)
        fc_bias_other = biases_other[width:]
        thoughts_core = flip(thoughts[0])
        near = jnp.where(core == side, thoughts[0], thoughts_core)
        far = cross(jnp.where(core == side, thoughts_core, thoughts[0]))
        thought_rows = join(side, near, far, axis=1)
        latent_core = flip(latent_pos)
        latent = jnp.where(core == side, latent_pos, latent_core)[0]
        full_cot = deal(cotangent)

        local = jnp.arange(rows, dtype=jnp.int32)
        positions = (2 * (local // block) + core) * block + local % block
        length = lengths[dealing[slot]]
        info = jnp.stack([core, length]).astype(jnp.int32)
        valid = (positions < length).astype(F32)[:, None]

        hit = positions[:, None] == latent[None, :]
        placed = jnp.dot(hit.astype(BF16), thought_rows, preferred_element_type=F32)
        inputs = jnp.where(jnp.any(hit, axis=-1, keepdims=True), placed, dealt.astype(F32))
        xhat_in, rstd_in = normalize(inputs)
        normed = (xhat_in * norm_gain[0] + norm_shift[0]).astype(BF16)

        def project(index, bias):
            own = dot_nn(normed, qkv_weight[index])
            other = dot_nn(normed, qkv_other[index])
            if bias is not None:
                own, other = own + qv_bias[bias], other + qv_other[bias]
            return jnp.concatenate([own.astype(BF16), other.astype(BF16)], axis=1)

        keys_own = project(1, None)
        keys_other = flip(keys_own)
        values_own = project(2, 1)
        values_other = flip(values_own)
        queries = project(0, 0)
        heads_out, lse = attend_forward(info, block, queries, keys_own, values_own, keys_other, values_other)
        residual = inputs + (
            dot_nn(heads_out[:, :half_width], out_weight) + dot_nn(heads_out[:, half_width:], out_other) + out_bias[0]
        )
        xhat_mid, rstd_mid = normalize(residual)
        normed_mlp = (xhat_mid * norm_gain[1] + norm_shift[1]).astype(BF16)
        grad_out = valid * full_cot.astype(F32)
        grad_mlp = grad_out.astype(BF16)

        mlp = jnp.zeros((rows, width), F32)
        grad_normed_mlp = jnp.zeros((rows, width), F32)
        grad_proj, grad_fc, grad_fc_bias = [], [], []
        for fc, bias, proj in ((fc_weight, fc_bias, proj_weight), (fc_other, fc_bias_other, proj_other)):
            active, slope = gelu_and_slope(dot_nn(normed_mlp, fc) + bias)
            active = active.astype(BF16)
            mlp = mlp + dot_nn(active, proj)
            grad_proj.append(dot_tn(active, grad_mlp))
            grad_pre = (dot_nt(grad_mlp, proj) * slope).astype(BF16)
            grad_fc.append(dot_tn(normed_mlp, grad_pre))
            grad_fc_bias.append(jnp.sum(grad_pre.astype(F32), axis=0))
            grad_normed_mlp = grad_normed_mlp + dot_nt(grad_pre, fc)
        block_out = undeal(valid * (residual + (mlp + out_bias[1])))

        def reduce_weight(own, other):
            kept_own = part(own, core) + flip(part(own, 1 - core).astype(BF16)).astype(F32)
            kept_other = part(other, core) + flip(part(other, 1 - core).astype(BF16)).astype(F32)
            total = kept_own + cross(kept_other.astype(BF16)).astype(F32)
            for bit in range(1, bits):
                flag = (group >> bit) & 1
                total = part(total, flag) + flip(part(total, 1 - flag).astype(BF16), bit).astype(F32)
            piece = total.astype(BF16)
            for bit in reversed(range(bits)):
                flag = (group >> bit) & 1
                piece = join(flag, piece, flip(piece, bit))
            return piece.astype(F32)

        def reduce_small(vectors):
            total = jnp.concatenate(vectors)
            total = total + cross(total)
            for bit in range(bits):
                total = total + flip(total, bit)
            return total

        def own_half(vector, halves):
            return lax.dynamic_slice_in_dim(vector, side * halves, halves, vector.ndim - 1)

        grad_proj_weight = reduce_weight(*grad_proj)
        grad_fc_weight = reduce_weight(*grad_fc)
        row_grad, gain_mlp, shift_mlp = norm_back(grad_normed_mlp, norm_gain[1], xhat_mid, rstd_mid)
        grad_residual = grad_out + row_grad
        small_mlp = reduce_small(
            [join(side, grad_fc_bias[0], grad_fc_bias[1]), jnp.sum(grad_mlp.astype(F32), axis=0), gain_mlp, shift_mlp]
        )

        grad_attn = grad_residual.astype(BF16)
        grad_out_weight = reduce_weight(
            dot_tn(heads_out[:, :half_width], grad_attn), dot_tn(heads_out[:, half_width:], grad_attn)
        )
        grad_heads = jnp.concatenate(
            [dot_nt(grad_attn, out_weight).astype(BF16), dot_nt(grad_attn, out_other).astype(BF16)], axis=1
        )
        grad_q, grad_ko, grad_vo, grad_kx, grad_vx = attend_backward(
            info, block, queries, keys_own, values_own, keys_other, values_other, grad_heads, heads_out, lse
        )
        grad_k = (grad_ko + flip(grad_kx).astype(F32)).astype(BF16)
        grad_v = (grad_vo + flip(grad_vx).astype(F32)).astype(BF16)
        triple = (grad_q, grad_k, grad_v)
        grad_qkv = [
            jnp.concatenate([dot_tn(normed, rows_grad[:, lanes]) for rows_grad in triple], axis=0)
            for lanes in (slice(0, half_width), slice(half_width, width))
        ]
        grad_qkv_weight = reduce_weight(*grad_qkv).reshape(3, width, half_width)
        grad_normed = jnp.zeros((rows, width), F32)
        for index, rows_grad in enumerate(triple):
            grad_normed = grad_normed + (
                dot_nt(rows_grad[:, :half_width], qkv_weight[index])
                + dot_nt(rows_grad[:, half_width:], qkv_other[index])
            )
        row_grad, gain_attn, shift_attn = norm_back(grad_normed, norm_gain[0], xhat_in, rstd_in)
        input_grad = undeal(grad_residual + row_grad)

        def ordered(vector):
            return join(side, vector[:half_width], vector[half_width:])

        small_attn = reduce_small(
            [
                ordered(jnp.sum(grad_q.astype(F32), axis=0)),
                ordered(jnp.sum(grad_v.astype(F32), axis=0)),
                jnp.sum(grad_attn.astype(F32), axis=0),
                gain_attn,
                shift_attn,
            ]
        )
        hidden = 2 * hidden_half
        grad_fc_bias = own_half(small_mlp[:hidden], hidden_half)
        bias_mlp, gain_mlp, shift_mlp = small_mlp[hidden:].reshape(3, width)
        grad_qv_bias = own_half(small_attn[: 2 * width].reshape(2, width), half_width)
        bias_attn, gain_attn, shift_attn = small_attn[2 * width :].reshape(3, width)
        return (
            block_out,
            input_grad,
            grad_qkv_weight,
            grad_qv_bias,
            grad_out_weight,
            jnp.stack([bias_attn, bias_mlp]),
            grad_fc_weight,
            grad_fc_bias,
            grad_proj_weight,
            jnp.stack([gain_attn, gain_mlp]),
            jnp.stack([shift_attn, shift_mlp]),
        )

    return jax.shard_map(
        body,
        mesh=mesh,
        in_specs=(
            P(None, "dp", "tensor"),
            P(None, "dp", "tensor"),
            P("dp", None, "tensor"),
            P("dp", None),
            P(),
            P(),
            P(None, None, "tensor"),
            P(None, "tensor"),
            P("tensor", None),
            P(),
            P(None, "tensor"),
            P("tensor"),
            P("tensor", None),
            P(),
            P(),
        ),
        out_specs=(
            P(None, "dp", "tensor"),
            P(None, "dp", "tensor"),
            P(None, None, "tensor"),
            P(None, "tensor"),
            P("tensor", None),
            P(),
            P(None, "tensor"),
            P("tensor"),
            P("tensor", None),
            P(),
            P(),
        ),
        check_vma=False,
    )
```

time: 1030 us -> 542 us (0.53)
  waiting for transfers between devices: 524 us -> 205 us
  blocking collectives: 170 us -> 0 us
  starting transfers between devices: 17.6 us -> 86.5 us
  matrix products: 132 us -> 74.9 us
  local copies, waits for them, and re-layouts: 104 us -> 59.7 us
  Pallas kernels: 0 us -> 36.9 us
  between operations: 19.5 us -> 4.48 us
    unnamed x12 -> x0, waiting for transfers between devices: 241 us -> none
    ppermute x0 -> x66, waiting for transfers between devices: none -> 192 us  [the longest x12 111 us: cross(): return lax.ppermute(value, AXES, tensor_pairs)]
    psum x3 -> x0, waiting for transfers between devices: 186 us -> none  [the longest x1 75.2 us: body(): lax.psum(jnp.einsum('cre,cde->rd', grad_qkv_rows, qkv_weight, preferred_e...]
    unnamed x2 -> x0, blocking collectives: 138 us -> none
    ppermute x0 -> x66, starting transfers between devices: none -> 61.1 us  [the longest x54 47 us: flip(): return lax.ppermute(value, AXES, bit_pairs[bit])]
    all_gather x6 -> x0, waiting for transfers between devices: 58.8 us -> none  [the longest x1 22.3 us: body(): lax.all_gather(summed[0], 'dp', axis=0, tiled=True)]
    dot_general x25 -> x37, matrix products: 132 us -> 74.9 us  [the longest x12 25.6 us: dot_nt(): lax.dot_general(left, right, (((1,), (1,)), ((), ())), preferred_element_...]
    reshape x11 -> x5, local copies, waits for them, and re-layouts: 47.6 us -> 4.31 us  [the longest x4 4.3 us: undeal(): array.astype(BF16).reshape(slots // 2, block, 2, half_width)]
  transfers between devices with their start and end apart: 14 -> 70, of which waited for: 9 -> 25; matrix products, arithmetic and copies ran while one was open for 12% -> 26% of each run, Pallas kernels for 0% -> 3%
where the time goes in v1:
time: 542 us; the launch traced here: 532 us
  waiting for transfers between devices  205 us (38%)
  starting transfers between devices  86.5 us (16%)
  matrix products  74.9 us (14%)
  other arithmetic  64.6 us (12%)
  local copies, waits for them, and re-layouts  59.7 us (11%)
  Pallas kernels  36.9 us (7%)
    ppermute x12, waiting for transfers between devices, cross(): return lax.ppermute(value, AXES, tensor_pairs)  111 us
    ppermute x54, waiting for transfers between devices, flip(): return lax.ppermute(value, AXES, bit_pairs[bit])  81.1 us
    ppermute x54, starting transfers between devices, flip(): return lax.ppermute(value, AXES, bit_pairs[bit])  47 us
    dot_general x12, matrix products, dot_nt(): lax.dot_general(left, right, (((1,), (1,)), ((), ())), preferred_element_...  25.6 us
    dot_general x12, matrix products, dot_tn(): lax.dot_general(left, right, (((0,), (0,)), ((), ())), preferred_element_...  24.9 us
    dot_general x12, matrix products, dot_nn(): lax.dot_general(left, right, (((1,), (0,)), ((), ())), preferred_element_...  23.8 us
    pallas_call x1, Pallas kernels, attend_backward(): pl.pallas_call(functools.partial(attend_backward_kernel, tile, block), gr...  21.3 us
    pallas_call x1, Pallas kernels, attend_forward(): pl.pallas_call(functools.partial(attend_forward_kernel, tile, block), gri...  15.6 us
  transfers between devices with their start and end apart: 70, of which 25 were waited for; matrix products, arithmetic and copies ran while one was open for 26% of the time, Pallas kernels for 3%

profile of v1, /device:TPU:0, one launch (start us, length us, event | category | flops | bytes accessed | tf_op | source)
XLA Modules:
  0.0 531.9 jit_solution(5490903393103832951)
XLA Ops:
  2.0 2.7 gather_fusion
  4.7 8.3 %all-to-all-start = ((bf16[16,64,384]{2,1,0:T(8,128)(2,1)}), bf16[16,64,384]{2,1,0:T(8,128)(2,1)S(1)}, u32[]{:S(2)}, u32[]{:S(2)}) async-start(bf16[16,64,384]{2,1,0:T(8,128)(2,1)} %gather_fusion), calls=%async_computation | async-start | bytes 1572864 | tf_op jit(solution)/shard_map/all_to_all | solution.py:263
  30.3 2.7 gather_fusion.2
  38.0 57.1 %collective-permute-done.5 = f32[2304]{0:T(1024)S(1)} collective-permute-done((f32[2304]{0:T(1024)S(1)}, f32[2304]{0:T(1024)S(1)}, u32[]{:S(2)}, u32[]{:S(2)}) %collective-permute-start.5) | collective-permute-done | bytes 9248 | tf_op jit(solution)/shard_map/ppermute | solution.py:242
  101.4 5.7 %all-to-all-start.2 = ((bf16[16,64,384]{2,1,0:T(8,128)(2,1)}), bf16[16,64,384]{2,1,0:T(8,128)(2,1)}, u32[]{:S(2)}, u32[]{:S(2)}) async-start(bf16[16,64,384]{2,1,0:T(8,128)(2,1)} %gather_fusion.2), calls=%async_computation.2 | async-start | bytes 1572864 | tf_op jit(solution)/shard_map/all_to_all | solution.py:263
  114.0 13.1 %all-to-all-done.2 = bf16[16,64,384]{2,1,0:T(8,128)(2,1)} async-done(((bf16[16,64,384]{2,1,0:T(8,128)(2,1)}), bf16[16,64,384]{2,1,0:T(8,128)(2,1)}, u32[]{:S(2)}, u32[]{:S(2)}) %all-to-all-start.2) | async-done | bytes 786464 | tf_op jit(solution)/shard_map/all_to_all | solution.py:263
  145.2 15.6 %attend_forward.1 = (bf16[512,768]{1,0:T(8,128)(2,1)}, f32[6,2,512]{2,1,0:T(2,128)}) custom-call(s32[2]{0:T(128)} %pad_add_fusion.info, bf16[512,768]{1,0:T(8,128)(2,1)} %pad_maximum_fusion.2.q_ref, bf16[512,768]{1,0:T(8,128)(2,1)} %pad_maximum_fusion.3.ko_ref, bf16[512,768]{1,0:T(8,128)(2,1)} %pad_maximum_fusion.4.vo_ref, ...), custom_call_target="tpu_custom_call" | custom-call | tf_op jit(solution)/shard_map/attend_forward/pallas_call | solution.py:139
  168.5 3.9 fusion.102
  172.4 2.8 convert_reduce_fusion.1
  175.3 3.8 convolution_add_fusion
  180.5 4.0 fusion.101
  184.5 3.1 fusion.103
  187.7 5.4 %convert_reduce_fusion = (f32[1536]{0:T(1024)S(1)}, bf16[512,1536]{1,0:T(8,128)(2,1)S(1)}) fusion(f32[512,1536]{1,0:T(8,128)S(1)} %convolution_add_fusion, bf16[512,768]{1,0:T(8,128)(2,1)S(1)} %copy-done.35, bf16[768,768]{1,0:T(8,128)(2,1)} %collective-permute-done.13, bf16[768,768]{1,0:T(8,128)(2,1)} %collective-permute-done.12, pred[]{:T(512)S(6)} %eq.32), kind=kOutput, calls=%fused_computation.11 | convolution fusion | flops 1234303488 | bytes 7870465 | tf_op jit(solution)/shard_map/dot_general | solution.py:24
  193.1 4.6 multiply_reduce_fusion
  206.1 21.3 %attend_backward.1 = (bf16[512,768]{1,0:T(8,128)(2,1)}, f32[512,768]{1,0:T(8,128)}, f32[512,768]{1,0:T(8,128)}, bf16[512,768]{1,0:T(8,128)(2,1)}, bf16[512,768]{1,0:T(8,128)(2,1)}) custom-call(s32[2]{0:T(128)} %pad_add_fusion.info, bf16[512,768]{1,0:T(8,128)(2,1)} %pad_maximum_fusion.2.q_ref, bf16[512,768]{1,0:T(8,128)(2,1)} %pad_maximum_fusion.3.ko_ref, ...), custom_call_target="tpu_custom_call" | custom-call | tf_op jit(solution)/shard_map/attend_backward/pallas_call | solution.py:160
  227.4 2.7 fusion.47
  231.7 2.8 fusion.23
  234.5 3.0 fusion.15
  237.5 3.6 fusion.113
  241.1 3.6 fusion.112
  245.0 5.5 %multiply_convert_fusion.3 = bf16[512,768]{1,0:T(8,128)(2,1)} fusion(f32[512,768]{1,0:T(8,128)S(1)} %copy-done.6, f32[512,768]{1,0:T(8,128)S(1)} %copy-done.69, f32[768]{0:T(1024)S(1)} %copy-done.58, f32[512]{0:T(512)S(1)} %copy-done.43, bf16[768,768]{1,0:T(8,128)(2,1)} %collective-permute-done.13, bf16[768,768]{1,0:T(8,128)(2,1)} %collective-permute-done.12, ...), kind=kOutput, calls=%fused_computation.53 | convolution fusion | flops 1227620352 | bytes 9442305 | tf_op jit(solution)/shard_map/dot_general | solution.py:20
  253.6 5.4 %all-to-all-start.1 = ((bf16[16,64,384]{2,1,0:T(8,128)(2,1)}), bf16[16,64,384]{2,1,0:T(8,128)(2,1)}, u32[]{:S(2)}, u32[]{:S(2)}) async-start(bf16[16,64,384]{2,1,0:T(8,128)(2,1)} %bitcast.89), calls=%async_computation.1 | async-start | bytes 1572864 | tf_op jit(solution)/shard_map/all_to_all | solution.py:273
  259.0 2.9 dynamic-slice_convert_fusion
  264.5 2.8 dynamic-slice_convert_fusion.2
  267.3 2.8 dynamic-slice_convert_fusion.3
  273.0 2.8 dynamic-slice_convert_fusion.1
  316.2 2.6 collective-permute-start.30
  324.4 3.4 add_convert_fusion.1
  336.6 15.5 %collective-permute-done.58 = bf16[768,768]{1,0:T(8,128)(2,1)S(1)} collective-permute-done((bf16[768,768]{1,0:T(8,128)(2,1)S(1)}, bf16[768,768]{1,0:T(8,128)(2,1)S(1)}, u32[]{:S(2)}, u32[]{:S(2)}) %collective-permute-start.58) | collective-permute-done | bytes 1179680 | tf_op jit(solution)/shard_map/ppermute | solution.py:242
  354.2 2.7 convert_add_fusion
  358.4 19.1 %collective-permute-done.48 = bf16[384,1536]{1,0:T(8,128)(2,1)} collective-permute-done((bf16[384,1536]{1,0:T(8,128)(2,1)}, bf16[384,1536]{1,0:T(8,128)(2,1)}, u32[]{:S(2)}, u32[]{:S(2)}) %collective-permute-start.48) | collective-permute-done | bytes 1179680 | tf_op jit(solution)/shard_map/ppermute | solution.py:242
  380.9 14.9 %collective-permute-done.18 = bf16[1152,384]{1,0:T(8,128)(2,1)S(1)} collective-permute-done((bf16[1152,384]{1,0:T(8,128)(2,1)S(1)}, bf16[1152,384]{1,0:T(8,128)(2,1)S(1)}, u32[]{:S(2)}, u32[]{:S(2)}) %collective-permute-start.18) | collective-permute-done | bytes 884768 | tf_op jit(solution)/shard_map/ppermute | solution.py:242
  399.0 8.9 %collective-permute-done.19 = bf16[576,384]{1,0:T(8,128)(2,1)S(1)} collective-permute-done((bf16[576,384]{1,0:T(8,128)(2,1)S(1)}, bf16[576,384]{1,0:T(8,128)(2,1)S(1)}, u32[]{:S(2)}, u32[]{:S(2)}) %collective-permute-start.19) | collective-permute-done | bytes 442400 | tf_op jit(solution)/shard_map/ppermute | solution.py:245
  410.3 7.4 %collective-permute-done.20 = bf16[288,384]{1,0:T(8,128)(2,1)S(1)} collective-permute-done((bf16[288,384]{1,0:T(8,128)(2,1)S(1)}, bf16[288,384]{1,0:T(8,128)(2,1)S(1)}, u32[]{:S(2)}, u32[]{:S(2)}) %collective-permute-start.20) | collective-permute-done | bytes 221216 | tf_op jit(solution)/shard_map/ppermute | solution.py:245
  417.7 2.8 collective-permute-start.21
  420.9 3.6 collective-permute-done.50
  427.7 9.5 %collective-permute-done.61 = bf16[96,768]{1,0:T(8,128)(2,1)S(1)} collective-permute-done((bf16[96,768]{1,0:T(8,128)(2,1)S(1)}, bf16[96,768]{1,0:T(8,128)(2,1)S(1)}, u32[]{:S(2)}, u32[]{:S(2)}) %collective-permute-start.61) | collective-permute-done | bytes 147488 | tf_op jit(solution)/shard_map/ppermute | solution.py:245
  437.3 3.0 collective-permute-done.51
  440.5 6.6 %collective-permute-done.22 = bf16[144,384]{1,0:T(8,128)(2,1)S(1)} collective-permute-done((bf16[144,384]{1,0:T(8,128)(2,1)S(1)}, bf16[144,384]{1,0:T(8,128)(2,1)S(1)}, u32[]{:S(2)}, u32[]{:S(2)}) %collective-permute-start.22) | collective-permute-done | bytes 110624 | tf_op jit(solution)/shard_map/ppermute | solution.py:245
  447.2 3.4 collective-permute-start.23
  452.2 3.1 collective-permute-start.53
  458.3 4.9 collective-permute-done.63
  464.7 6.0 %all-to-all-start.3 = ((bf16[16,64,384]{2,1,0:T(8,128)(2,1)}), bf16[16,64,384]{2,1,0:T(8,128)(2,1)S(1)}, u32[]{:S(2)}, u32[]{:S(2)}) async-start(bf16[16,64,384]{2,1,0:T(8,128)(2,1)} %bitcast.16), calls=%async_computation.3 | async-start | bytes 1572864 | tf_op jit(solution)/shard_map/all_to_all | solution.py:273
  475.6 13.7 %collective-permute-done.64 = bf16[384,768]{1,0:T(8,128)(2,1)} collective-permute-done((bf16[384,768]{1,0:T(8,128)(2,1)S(1)}, bf16[384,768]{1,0:T(8,128)(2,1)}, u32[]{:S(2)}, u32[]{:S(2)}) %collective-permute-start.64) | collective-permute-done | bytes 589856 | tf_op jit(solution)/shard_map/ppermute | solution.py:245
  491.4 11.5 %collective-permute-done.39 = bf16[96,768]{1,0:T(8,128)(2,1)S(1)} collective-permute-done((bf16[96,768]{1,0:T(8,128)(2,1)S(1)}, bf16[96,768]{1,0:T(8,128)(2,1)S(1)}, u32[]{:S(2)}, u32[]{:S(2)}) %collective-permute-start.39) | collective-permute-done | bytes 147488 | tf_op jit(solution)/shard_map/ppermute | solution.py:245
  507.9 2.8 gather_fusion.1
  521.6 4.4 fusion.3
  526.1 5.3 %fusion.2 = f32[768,1536]{1,0:T(8,128)} fusion(bf16[384,1536]{1,0:T(8,128)(2,1)} %collective-permute-done.55, bf16[384,1536]{1,0:T(8,128)(2,1)} %maximum_select_fusion.6, pred[]{:T(512)S(6)} %eq.33), kind=kLoop, calls=%fused_computation.22 | loop fusion | flops 11796480 | bytes 7077889 | tf_op jit(solution)/shard_map/convert_element_type | solution.py:354
  (437 shorter events, 180.2 us)
Async XLA Ops:
  0.7 35.2 %collective-permute-start = (s32[1,6]{1,0:T(1,128)}, s32[1,6]{1,0:T(1,128)S(1)}, u32[]{:S(2)}, u32[]{:S(2)}) collective-permute-start(s32[1,6]{1,0:T(1,128)} %param.18), channel_id=1, source_target_pairs={{0,2},{1,3},{2,0},{3,1},{4,6},{5,7},{6,4},{7,5},{8,10},{9,11},{10,... | collective-permute-start | bytes 80 | tf_op jit(solution)/shard_map/ppermute | solution.py:245
  1.2 34.8 %collective-permute-start.1 = (bf16[6,384]{1,0:T(8,128)(2,1)}, bf16[6,384]{1,0:T(8,128)(2,1)S(1)}, u32[]{:S(2)}, u32[]{:S(2)}) collective-permute-start(bf16[6,384]{1,0:T(8,128)(2,1)} %bitcast.91), channel_id=1, source_target_pairs={{0,2},{1,3},{2,0},{3,1},{4,6},{5,7},{6,4},{7,5},{8,10},{9,11},{10,... | collective-permute-start | bytes 13832 | tf_op jit(solution)/shard_map/ppermute | solution.py:245
  4.7 96.7 %all-to-all-start = ((bf16[16,64,384]{2,1,0:T(8,128)(2,1)}), bf16[16,64,384]{2,1,0:T(8,128)(2,1)S(1)}, u32[]{:S(2)}, u32[]{:S(2)}) async-start(bf16[16,64,384]{2,1,0:T(8,128)(2,1)} %gather_fusion), calls=%async_computation | async-start | bytes 1572864 | tf_op jit(solution)/shard_map/all_to_all | solution.py:263
  15.2 85.1 %collective-permute-start.3 = (bf16[1152,384]{1,0:T(8,128)(2,1)}, bf16[1152,384]{1,0:T(8,128)(2,1)}, u32[]{:S(2)}, u32[]{:S(2)}) collective-permute-start(bf16[1152,384]{1,0:T(8,128)(2,1)} %constant_dynamic-slice_fusion.4), channel_id=1, source_target_pairs={{0,1},{1,0},{2,3},{3,2},{4,5},{5,4},{6,7},{7,6},{8,9},{9,8},{10,11... | collective-permute-start | bytes 2654216 | tf_op jit(solution)/shard_map/ppermute | solution.py:242
  18.3 82.6 %collective-permute-start.12 = (bf16[768,768]{1,0:T(8,128)(2,1)}, bf16[768,768]{1,0:T(8,128)(2,1)}, u32[]{:S(2)}, u32[]{:S(2)}) collective-permute-start(bf16[768,768]{1,0:T(8,128)(2,1)} %constant_dynamic-slice_fusion.1), channel_id=1, source_target_pairs={{0,1},{1,0},{2,3},{3,2},{4,5},{5,4},{6,7},{7,6},{8,9},{9,8},{10,11... | collective-permute-start | bytes 3538952 | tf_op jit(solution)/shard_map/ppermute | solution.py:242
  20.8 80.1 %collective-permute-start.10 = (bf16[384,1536]{1,0:T(8,128)(2,1)}, bf16[384,1536]{1,0:T(8,128)(2,1)}, u32[]{:S(2)}, u32[]{:S(2)}) collective-permute-start(bf16[384,1536]{1,0:T(8,128)(2,1)} %constant_dynamic-slice_fusion.2), channel_id=1, source_target_pairs={{0,1},{1,0},{2,3},{3,2},{4,5},{5,4},{6,7},{7,6},{8,9},{9,8},{10,11... | collective-permute-start | bytes 3538952 | tf_op jit(solution)/shard_map/ppermute | solution.py:242
  35.8 59.3 %collective-permute-start.5 = (f32[2304]{0:T(1024)S(1)}, f32[2304]{0:T(1024)S(1)}, u32[]{:S(2)}, u32[]{:S(2)}) collective-permute-start(f32[2304]{0:T(1024)S(1)} %pad_maximum_fusion.7), channel_id=1, source_target_pairs={{0,1},{1,0},{2,3},{3,2},{4,5},{5,4},{6,7},{7,6},{8,9},{9,8},{10,11... | collective-permute-start | bytes 27656 | tf_op jit(solution)/shard_map/ppermute | solution.py:242
  36.1 64.3 %collective-permute-start.8 = (bf16[192,768]{1,0:T(8,128)(2,1)S(1)}, bf16[192,768]{1,0:T(8,128)(2,1)}, u32[]{:S(2)}, u32[]{:S(2)}) collective-permute-start(bf16[192,768]{1,0:T(8,128)(2,1)S(1)} %constant_dynamic-slice_fusion.3), channel_id=1, source_target_pairs={{0,1},{1,0},{2,3},{3,2},{4,5},{5,4},{6,7},{7,6},{8,9},{9,8},{10,11... | collective-permute-start | bytes 884744 | tf_op jit(solution)/shard_map/ppermute | solution.py:242
  95.1 12.9 %collective-permute-start.2 = (bf16[6,384]{1,0:T(8,128)(2,1)S(1)}, bf16[6,384]{1,0:T(8,128)(2,1)S(1)}, u32[]{:S(2)}, u32[]{:S(2)}) collective-permute-start(bf16[6,384]{1,0:T(8,128)(2,1)S(1)} %get-tuple-element.55), channel_id=1, source_target_pairs={{0,1},{1,0},{2,3},{3,2},{4,5},{5,4},{6,7},{7,6},{8,9},{9,8},{10,11... | collective-permute-start | bytes 13832 | tf_op jit(solution)/shard_map/ppermute | solution.py:242
  100.4 62.4 %collective-permute-start.9 = (bf16[192,768]{1,0:T(8,128)(2,1)}, bf16[192,768]{1,0:T(8,128)(2,1)}, u32[]{:S(2)}, u32[]{:S(2)}) collective-permute-start(bf16[192,768]{1,0:T(8,128)(2,1)} %collective-permute-done.8), channel_id=1, source_target_pairs={{0,2},{1,3},{2,0},{3,1},{4,6},{5,7},{6,4},{7,5},{8,10},{9,11},{10,... | collective-permute-start | bytes 884744 | tf_op jit(solution)/shard_map/ppermute | solution.py:245
  100.4 29.2 %collective-permute-start.4 = (bf16[1152,384]{1,0:T(8,128)(2,1)}, bf16[1152,384]{1,0:T(8,128)(2,1)}, u32[]{:S(2)}, u32[]{:S(2)}) collective-permute-start(bf16[1152,384]{1,0:T(8,128)(2,1)} %collective-permute-done.3), channel_id=1, source_target_pairs={{0,2},{1,3},{2,0},{3,1},{4,6},{5,7},{6,4},{7,5},{8,10},{9,11},{10,... | collective-permute-start | bytes 2654216 | tf_op jit(solution)/shard_map/ppermute | solution.py:245
  100.9 86.8 %collective-permute-start.13 = (bf16[768,768]{1,0:T(8,128)(2,1)}, bf16[768,768]{1,0:T(8,128)(2,1)}, u32[]{:S(2)}, u32[]{:S(2)}) collective-permute-start(bf16[768,768]{1,0:T(8,128)(2,1)} %collective-permute-done.12), channel_id=1, source_target_pairs={{0,2},{1,3},{2,0},{3,1},{4,6},{5,7},{6,4},{7,5},{8,10},{9,11},{10,... | collective-permute-start | bytes 3538952 | tf_op jit(solution)/shard_map/ppermute | solution.py:245
  100.9 74.3 %collective-permute-start.11 = (bf16[384,1536]{1,0:T(8,128)(2,1)}, bf16[384,1536]{1,0:T(8,128)(2,1)}, u32[]{:S(2)}, u32[]{:S(2)}) collective-permute-start(bf16[384,1536]{1,0:T(8,128)(2,1)} %collective-permute-done.10), channel_id=1, source_target_pairs={{0,2},{1,3},{2,0},{3,1},{4,6},{5,7},{6,4},{7,5},{8,10},{9,11},{10,... | collective-permute-start | bytes 3538952 | tf_op jit(solution)/shard_map/ppermute | solution.py:245
  101.4 25.7 %all-to-all-start.2 = ((bf16[16,64,384]{2,1,0:T(8,128)(2,1)}), bf16[16,64,384]{2,1,0:T(8,128)(2,1)}, u32[]{:S(2)}, u32[]{:S(2)}) async-start(bf16[16,64,384]{2,1,0:T(8,128)(2,1)} %gather_fusion.2), calls=%async_computation.2 | async-start | bytes 1572864 | tf_op jit(solution)/shard_map/all_to_all | solution.py:263
  253.6 211.1 %all-to-all-start.1 = ((bf16[16,64,384]{2,1,0:T(8,128)(2,1)}), bf16[16,64,384]{2,1,0:T(8,128)(2,1)}, u32[]{:S(2)}, u32[]{:S(2)}) async-start(bf16[16,64,384]{2,1,0:T(8,128)(2,1)} %bitcast.89), calls=%async_computation.1 | async-start | bytes 1572864 | tf_op jit(solution)/shard_map/all_to_all | solution.py:273
  261.9 59.0 %collective-permute-start.57 = (bf16[768,768]{1,0:T(8,128)(2,1)}, bf16[768,768]{1,0:T(8,128)(2,1)}, u32[]{:S(2)}, u32[]{:S(2)}) collective-permute-start(bf16[768,768]{1,0:T(8,128)(2,1)} %dynamic-slice_convert_fusion), channel_id=1, source_target_pairs={{0,2},{1,3},{2,0},{3,1},{4,6},{5,7},{6,4},{7,5},{8,10},{9,11},{10,... | collective-permute-start | bytes 3538952 | tf_op jit(solution)/shard_map/ppermute | solution.py:245
  264.0 20.5 %collective-permute-start.31 = (bf16[192,768]{1,0:T(8,128)(2,1)S(1)}, bf16[192,768]{1,0:T(8,128)(2,1)S(1)}, u32[]{:S(2)}, u32[]{:S(2)}) collective-permute-start(bf16[192,768]{1,0:T(8,128)(2,1)S(1)} %dynamic-slice_convert_fusion.12), channel_id=1, source_target_pairs={{0,2},{1,3},{2,0},{3,1},{4,6},{5,7},{6,4},{7,5},{8,10},{9,11},{10,... | collective-permute-start | bytes 884744 | tf_op jit(solution)/shard_map/ppermute | solution.py:245
  264.2 13.1 %collective-permute-start.32 = (bf16[192,768]{1,0:T(8,128)(2,1)S(1)}, bf16[192,768]{1,0:T(8,128)(2,1)S(1)}, u32[]{:S(2)}, u32[]{:S(2)}) collective-permute-start(bf16[192,768]{1,0:T(8,128)(2,1)S(1)} %dynamic-slice_convert_fusion.11), channel_id=1, source_target_pairs={{0,2},{1,3},{2,0},{3,1},{4,6},{5,7},{6,4},{7,5},{8,10},{9,11},{10,... | collective-permute-start | bytes 884744 | tf_op jit(solution)/shard_map/ppermute | solution.py:245
  275.8 58.2 %collective-permute-start.56 = (bf16[768,768]{1,0:T(8,128)(2,1)}, bf16[768,768]{1,0:T(8,128)(2,1)}, u32[]{:S(2)}, u32[]{:S(2)}) collective-permute-start(bf16[768,768]{1,0:T(8,128)(2,1)} %dynamic-slice_convert_fusion.1), channel_id=1, source_target_pairs={{0,2},{1,3},{2,0},{3,1},{4,6},{5,7},{6,4},{7,5},{8,10},{9,11},{10,... | collective-permute-start | bytes 3538952 | tf_op jit(solution)/shard_map/ppermute | solution.py:245
  291.9 32.4 %collective-permute-start.47 = (bf16[384,1536]{1,0:T(8,128)(2,1)}, bf16[384,1536]{1,0:T(8,128)(2,1)}, u32[]{:S(2)}, u32[]{:S(2)}) collective-permute-start(bf16[384,1536]{1,0:T(8,128)(2,1)} %dynamic-slice_convert_fusion.2), channel_id=1, source_target_pairs={{0,2},{1,3},{2,0},{3,1},{4,6},{5,7},{6,4},{7,5},{8,10},{9,11},{10,... | collective-permute-start | bytes 3538952 | tf_op jit(solution)/shard_map/ppermute | solution.py:245
  292.0 15.7 %collective-permute-start.35 = (bf16[48,768]{1,0:T(8,128)(2,1)S(1)}, bf16[48,768]{1,0:T(8,128)(2,1)S(1)}, u32[]{:S(2)}, u32[]{:S(2)}) collective-permute-start(bf16[48,768]{1,0:T(8,128)(2,1)S(1)} %dynamic-slice_convert_fusion.18), channel_id=1, source_target_pairs={{0,8},{1,9},{2,10},{3,11},{4,12},{5,13},{6,14},{7,15},{8,0},{9,1},... | collective-permute-start | bytes 221192 | tf_op jit(solution)/shard_map/ppermute | solution.py:245
  316.2 40.8 %collective-permute-start.46 = (bf16[384,1536]{1,0:T(8,128)(2,1)}, bf16[384,1536]{1,0:T(8,128)(2,1)S(1)}, u32[]{:S(2)}, u32[]{:S(2)}) collective-permute-start(bf16[384,1536]{1,0:T(8,128)(2,1)} %dynamic-slice_convert_fusion.3), channel_id=1, source_target_pairs={{0,2},{1,3},{2,0},{3,1},{4,6},{5,7},{6,4},{7,5},{8,10},{9,11},{10,... | collective-permute-start | bytes 3538952 | tf_op jit(solution)/shard_map/ppermute | solution.py:245
  323.2 28.9 %collective-permute-start.58 = (bf16[768,768]{1,0:T(8,128)(2,1)S(1)}, bf16[768,768]{1,0:T(8,128)(2,1)S(1)}, u32[]{:S(2)}, u32[]{:S(2)}) collective-permute-start(bf16[768,768]{1,0:T(8,128)(2,1)S(1)} %add_convert_fusion), channel_id=1, source_target_pairs={{0,1},{1,0},{2,3},{3,2},{4,5},{5,4},{6,7},{7,6},{8,9},{9,8},{10,11... | collective-permute-start | bytes 3538952 | tf_op jit(solution)/shard_map/ppermute | solution.py:242
  327.8 49.7 %collective-permute-start.48 = (bf16[384,1536]{1,0:T(8,128)(2,1)}, bf16[384,1536]{1,0:T(8,128)(2,1)}, u32[]{:S(2)}, u32[]{:S(2)}) collective-permute-start(bf16[384,1536]{1,0:T(8,128)(2,1)} %add_convert_fusion.1), channel_id=1, source_target_pairs={{0,1},{1,0},{2,3},{3,2},{4,5},{5,4},{6,7},{7,6},{8,9},{9,8},{10,11... | collective-permute-start | bytes 3538952 | tf_op jit(solution)/shard_map/ppermute | solution.py:242
  331.9 49.1 %collective-permute-start.16 = (bf16[1152,384]{1,0:T(8,128)(2,1)}, bf16[1152,384]{1,0:T(8,128)(2,1)S(1)}, u32[]{:S(2)}, u32[]{:S(2)}) collective-permute-start(bf16[1152,384]{1,0:T(8,128)(2,1)} %dynamic-slice_convert_fusion.5), channel_id=1, source_target_pairs={{0,2},{1,3},{2,0},{3,1},{4,6},{5,7},{6,4},{7,5},{8,10},{9,11},{10,... | collective-permute-start | bytes 2654216 | tf_op jit(solution)/shard_map/ppermute | solution.py:245
  334.0 121.3 %collective-permute-start.37 = (bf16[24,768]{1,0:T(8,128)(2,1)S(1)}, bf16[24,768]{1,0:T(8,128)(2,1)S(1)}, u32[]{:S(2)}, u32[]{:S(2)}) collective-permute-start(bf16[24,768]{1,0:T(8,128)(2,1)S(1)} %copy-done.39), channel_id=1, source_target_pairs={{0,16},{1,17},{2,18},{3,19},{4,20},{5,21},{6,22},{7,23},{8,24},{9,... | collective-permute-start | bytes 110600 | tf_op jit(solution)/shard_map/ppermute | solution.py:245
  353.1 42.7 %collective-permute-start.18 = (bf16[1152,384]{1,0:T(8,128)(2,1)S(1)}, bf16[1152,384]{1,0:T(8,128)(2,1)S(1)}, u32[]{:S(2)}, u32[]{:S(2)}) collective-permute-start(bf16[1152,384]{1,0:T(8,128)(2,1)S(1)} %add_convert_fusion.2), channel_id=1, source_target_pairs={{0,1},{1,0},{2,3},{3,2},{4,5},{5,4},{6,7},{7,6},{8,9},{9,8},{10,11... | collective-permute-start | bytes 2654216 | tf_op jit(solution)/shard_map/ppermute | solution.py:242
  357.0 40.5 %collective-permute-start.59 = (bf16[384,768]{1,0:T(8,128)(2,1)S(1)}, bf16[384,768]{1,0:T(8,128)(2,1)S(1)}, u32[]{:S(2)}, u32[]{:S(2)}) collective-permute-start(bf16[384,768]{1,0:T(8,128)(2,1)S(1)} %dynamic-slice_convert_fusion.6), channel_id=1, source_target_pairs={{0,4},{1,5},{2,6},{3,7},{4,0},{5,1},{6,2},{7,3},{8,12},{9,13},{10,... | collective-permute-start | bytes 1769480 | tf_op jit(solution)/shard_map/ppermute | solution.py:245
  379.6 19.3 %collective-permute-start.49 = (bf16[192,1536]{1,0:T(8,128)(2,1)S(1)}, bf16[192,1536]{1,0:T(8,128)(2,1)S(1)}, u32[]{:S(2)}, u32[]{:S(2)}) collective-permute-start(bf16[192,1536]{1,0:T(8,128)(2,1)S(1)} %dynamic-slice_convert_fusion.7), channel_id=1, source_target_pairs={{0,4},{1,5},{2,6},{3,7},{4,0},{5,1},{6,2},{7,3},{8,12},{9,13},{10,... | collective-permute-start | bytes 1769480 | tf_op jit(solution)/shard_map/ppermute | solution.py:245
  396.2 11.8 %collective-permute-start.19 = (bf16[576,384]{1,0:T(8,128)(2,1)S(1)}, bf16[576,384]{1,0:T(8,128)(2,1)S(1)}, u32[]{:S(2)}, u32[]{:S(2)}) collective-permute-start(bf16[576,384]{1,0:T(8,128)(2,1)S(1)} %dynamic-slice_convert_fusion.8), channel_id=1, source_target_pairs={{0,4},{1,5},{2,6},{3,7},{4,0},{5,1},{6,2},{7,3},{8,12},{9,13},{10,... | collective-permute-start | bytes 1327112 | tf_op jit(solution)/shard_map/ppermute | solution.py:245
  398.0 22.6 %collective-permute-start.60 = (bf16[192,768]{1,0:T(8,128)(2,1)S(1)}, bf16[192,768]{1,0:T(8,128)(2,1)S(1)}, u32[]{:S(2)}, u32[]{:S(2)}) collective-permute-start(bf16[192,768]{1,0:T(8,128)(2,1)S(1)} %dynamic-slice_convert_fusion.9), channel_id=1, source_target_pairs={{0,8},{1,9},{2,10},{3,11},{4,12},{5,13},{6,14},{7,15},{8,0},{9,1},... | collective-permute-start | bytes 884744 | tf_op jit(solution)/shard_map/ppermute | solution.py:245
  409.7 14.8 %collective-permute-start.50 = (bf16[96,1536]{1,0:T(8,128)(2,1)S(1)}, bf16[96,1536]{1,0:T(8,128)(2,1)S(1)}, u32[]{:S(2)}, u32[]{:S(2)}) collective-permute-start(bf16[96,1536]{1,0:T(8,128)(2,1)S(1)} %dynamic-slice_convert_fusion.10), channel_id=1, source_target_pairs={{0,8},{1,9},{2,10},{3,11},{4,12},{5,13},{6,14},{7,15},{8,0},{9,1},... | collective-permute-start | bytes 884744 | tf_op jit(solution)/shard_map/ppermute | solution.py:245
  420.7 16.6 %collective-permute-start.61 = (bf16[96,768]{1,0:T(8,128)(2,1)S(1)}, bf16[96,768]{1,0:T(8,128)(2,1)S(1)}, u32[]{:S(2)}, u32[]{:S(2)}) collective-permute-start(bf16[96,768]{1,0:T(8,128)(2,1)S(1)} %dynamic-slice_convert_fusion.14), channel_id=1, source_target_pairs={{0,16},{1,17},{2,18},{3,19},{4,20},{5,21},{6,22},{7,23},{8,24},{9,... | collective-permute-start | bytes 442376 | tf_op jit(solution)/shard_map/ppermute | solution.py:245
  424.6 15.8 %collective-permute-start.51 = (bf16[48,1536]{1,0:T(8,128)(2,1)S(1)}, bf16[48,1536]{1,0:T(8,128)(2,1)S(1)}, u32[]{:S(2)}, u32[]{:S(2)}) collective-permute-start(bf16[48,1536]{1,0:T(8,128)(2,1)S(1)} %dynamic-slice_convert_fusion.15), channel_id=1, source_target_pairs={{0,16},{1,17},{2,18},{3,19},{4,20},{5,21},{6,22},{7,23},{8,24},{9,... | collective-permute-start | bytes 442376 | tf_op jit(solution)/shard_map/ppermute | solution.py:245
  425.6 21.6 %collective-permute-start.22 = (bf16[144,384]{1,0:T(8,128)(2,1)S(1)}, bf16[144,384]{1,0:T(8,128)(2,1)S(1)}, u32[]{:S(2)}, u32[]{:S(2)}) collective-permute-start(bf16[144,384]{1,0:T(8,128)(2,1)S(1)} %add_convert_fusion.11), channel_id=1, source_target_pairs={{0,16},{1,17},{2,18},{3,19},{4,20},{5,21},{6,22},{7,23},{8,24},{9,... | collective-permute-start | bytes 331784 | tf_op jit(solution)/shard_map/ppermute | solution.py:245
  437.3 13.3 %collective-permute-start.62 = (bf16[96,768]{1,0:T(8,128)(2,1)S(1)}, bf16[96,768]{1,0:T(8,128)(2,1)S(1)}, u32[]{:S(2)}, u32[]{:S(2)}) collective-permute-start(bf16[96,768]{1,0:T(8,128)(2,1)S(1)} %add_convert_fusion.9), channel_id=1, source_target_pairs={{0,16},{1,17},{2,18},{3,19},{4,20},{5,21},{6,22},{7,23},{8,24},{9,... | collective-permute-start | bytes 442376 | tf_op jit(solution)/shard_map/ppermute | solution.py:245
  440.4 11.8 %collective-permute-start.52 = (bf16[48,1536]{1,0:T(8,128)(2,1)S(1)}, bf16[48,1536]{1,0:T(8,128)(2,1)S(1)}, u32[]{:S(2)}, u32[]{:S(2)}) collective-permute-start(bf16[48,1536]{1,0:T(8,128)(2,1)S(1)} %add_convert_fusion.10), channel_id=1, source_target_pairs={{0,16},{1,17},{2,18},{3,19},{4,20},{5,21},{6,22},{7,23},{8,24},{9,... | collective-permute-start | bytes 442376 | tf_op jit(solution)/shard_map/ppermute | solution.py:245
  450.7 12.6 %collective-permute-start.63 = (bf16[192,768]{1,0:T(8,128)(2,1)S(1)}, bf16[192,768]{1,0:T(8,128)(2,1)S(1)}, u32[]{:S(2)}, u32[]{:S(2)}) collective-permute-start(bf16[192,768]{1,0:T(8,128)(2,1)S(1)} %maximum_select_fusion.20), channel_id=1, source_target_pairs={{0,8},{1,9},{2,10},{3,11},{4,12},{5,13},{6,14},{7,15},{8,0},{9,1},... | collective-permute-start | bytes 884744 | tf_op jit(solution)/shard_map/ppermute | solution.py:245
  452.2 18.4 %collective-permute-start.53 = (bf16[96,1536]{1,0:T(8,128)(2,1)S(1)}, bf16[96,1536]{1,0:T(8,128)(2,1)}, u32[]{:S(2)}, u32[]{:S(2)}) collective-permute-start(bf16[96,1536]{1,0:T(8,128)(2,1)S(1)} %maximum_select_fusion.19), channel_id=1, source_target_pairs={{0,8},{1,9},{2,10},{3,11},{4,12},{5,13},{6,14},{7,15},{8,0},{9,1},... | collective-permute-start | bytes 884744 | tf_op jit(solution)/shard_map/ppermute | solution.py:245
  455.3 18.5 %collective-permute-start.38 = (bf16[48,768]{1,0:T(8,128)(2,1)S(1)}, bf16[48,768]{1,0:T(8,128)(2,1)S(1)}, u32[]{:S(2)}, u32[]{:S(2)}) collective-permute-start(bf16[48,768]{1,0:T(8,128)(2,1)S(1)} %maximum_select_fusion.25), channel_id=1, source_target_pairs={{0,8},{1,9},{2,10},{3,11},{4,12},{5,13},{6,14},{7,15},{8,0},{9,1},... | collective-permute-start | bytes 221192 | tf_op jit(solution)/shard_map/ppermute | solution.py:245
  457.1 17.0 %collective-permute-start.24 = (bf16[576,384]{1,0:T(8,128)(2,1)S(1)}, bf16[576,384]{1,0:T(8,128)(2,1)}, u32[]{:S(2)}, u32[]{:S(2)}) collective-permute-start(bf16[576,384]{1,0:T(8,128)(2,1)S(1)} %maximum_select_fusion.13), channel_id=1, source_target_pairs={{0,4},{1,5},{2,6},{3,7},{4,0},{5,1},{6,2},{7,3},{8,12},{9,13},{10,... | collective-permute-start | bytes 1327112 | tf_op jit(solution)/shard_map/ppermute | solution.py:245
  463.4 25.8 %collective-permute-start.64 = (bf16[384,768]{1,0:T(8,128)(2,1)S(1)}, bf16[384,768]{1,0:T(8,128)(2,1)}, u32[]{:S(2)}, u32[]{:S(2)}) collective-permute-start(bf16[384,768]{1,0:T(8,128)(2,1)S(1)} %maximum_select_fusion.12), channel_id=1, source_target_pairs={{0,4},{1,5},{2,6},{3,7},{4,0},{5,1},{6,2},{7,3},{8,12},{9,13},{10,... | collective-permute-start | bytes 1769480 | tf_op jit(solution)/shard_map/ppermute | solution.py:245
  464.7 48.4 %all-to-all-start.3 = ((bf16[16,64,384]{2,1,0:T(8,128)(2,1)}), bf16[16,64,384]{2,1,0:T(8,128)(2,1)S(1)}, u32[]{:S(2)}, u32[]{:S(2)}) async-start(bf16[16,64,384]{2,1,0:T(8,128)(2,1)} %bitcast.16), calls=%async_computation.3 | async-start | bytes 1572864 | tf_op jit(solution)/shard_map/all_to_all | solution.py:273
  471.9 31.2 %collective-permute-start.54 = (bf16[192,1536]{1,0:T(8,128)(2,1)S(1)}, bf16[192,1536]{1,0:T(8,128)(2,1)S(1)}, u32[]{:S(2)}, u32[]{:S(2)}) collective-permute-start(bf16[192,1536]{1,0:T(8,128)(2,1)S(1)} %maximum_select_fusion.11), channel_id=1, source_target_pairs={{0,4},{1,5},{2,6},{3,7},{4,0},{5,1},{6,2},{7,3},{8,12},{9,13},{10,... | collective-permute-start | bytes 1769480 | tf_op jit(solution)/shard_map/ppermute | solution.py:245
  473.9 29.0 %collective-permute-start.39 = (bf16[96,768]{1,0:T(8,128)(2,1)S(1)}, bf16[96,768]{1,0:T(8,128)(2,1)S(1)}, u32[]{:S(2)}, u32[]{:S(2)}) collective-permute-start(bf16[96,768]{1,0:T(8,128)(2,1)S(1)} %maximum_select_fusion.22), channel_id=1, source_target_pairs={{0,4},{1,5},{2,6},{3,7},{4,0},{5,1},{6,2},{7,3},{8,12},{9,13},{10,... | collective-permute-start | bytes 442376 | tf_op jit(solution)/shard_map/ppermute | solution.py:245
  475.5 41.7 %collective-permute-start.25 = (bf16[1152,384]{1,0:T(8,128)(2,1)S(1)}, bf16[1152,384]{1,0:T(8,128)(2,1)}, u32[]{:S(2)}, u32[]{:S(2)}) collective-permute-start(bf16[1152,384]{1,0:T(8,128)(2,1)S(1)} %maximum_select_fusion.8), channel_id=1, source_target_pairs={{0,2},{1,3},{2,0},{3,1},{4,6},{5,7},{6,4},{7,5},{8,10},{9,11},{10,... | collective-permute-start | bytes 2654216 | tf_op jit(solution)/shard_map/ppermute | solution.py:245
  491.3 30.3 %collective-permute-start.65 = (bf16[768,768]{1,0:T(8,128)(2,1)S(1)}, bf16[768,768]{1,0:T(8,128)(2,1)}, u32[]{:S(2)}, u32[]{:S(2)}) collective-permute-start(bf16[768,768]{1,0:T(8,128)(2,1)S(1)} %maximum_select_fusion.7), channel_id=1, source_target_pairs={{0,2},{1,3},{2,0},{3,1},{4,6},{5,7},{6,4},{7,5},{8,10},{9,11},{10,... | collective-permute-start | bytes 3538952 | tf_op jit(solution)/shard_map/ppermute | solution.py:245
  504.5 21.6 %collective-permute-start.55 = (bf16[384,1536]{1,0:T(8,128)(2,1)}, bf16[384,1536]{1,0:T(8,128)(2,1)}, u32[]{:S(2)}, u32[]{:S(2)}) collective-permute-start(bf16[384,1536]{1,0:T(8,128)(2,1)} %maximum_select_fusion.6), channel_id=1, source_target_pairs={{0,2},{1,3},{2,0},{3,1},{4,6},{5,7},{6,4},{7,5},{8,10},{9,11},{10,... | collective-permute-start | bytes 3538952 | tf_op jit(solution)/shard_map/ppermute | solution.py:245
  (94 other events, 679.9 us)
